TPU v7x, 32 devices: a whole 2x2x4 slice. The times are simulated.
32 devices in a mesh: row: 8 (over y, x, core), col: 4 (over z).
Axes of the slice: x: 2, y: 2, z: 4, core: 2. Of those that a mesh axis runs over, the one named last changes fastest.
Arguments:
- residual: float32 [8, 2048, 128], P(None, 'row'), may hold values from -6 to 6
- diag_inverse: bfloat16 [2, 2048, 2048], P(None, 'col', 'row'), as said below
- panels: bfloat16 [2, 8, 2048, 2048], P(None, None, 'row', 'col'), may hold values from -0.125 to 0.125
- first_block: int32 [1], replicated, may hold values from 0 to 6
- probe_solved: bfloat16 [8, 2048, 128], P(None, 'row'), may hold values from -6 to 6
- genotypes: bfloat16 [8, 2048, 16384], P(None, 'row', 'col'), may hold values from -6 to 6
- annotation: int32 [16384], P('col'), may hold values from 0 to 7
Outputs:
- trailing: float32 [8, 2048, 128], P(None, 'row')
- solved: float32 [2, 2048, 128], P(None, 'col')
- grm_products: bfloat16 [8, 2048, 8, 128], P(None, 'row', 'col')
Inputs may be any that keep to these rules, and one draw needn't show every extreme that they name: The two solve steps are blocks first_block and first_block + 1. diag_inverse is lower triangular in each of its two blocks.
All inputs are finite; a program needn't handle non-finite values.
Results may differ from a plain program's by a relative error of at most 0.0085.
Values may be sent and summed in bfloat16 or wider, within the bound.
No kernel may reach another device: no remote copies, remote signals or barrier semaphores. Data moves between devices by JAX's collectives and lax.ppermute only.
A program may use at most 128 MiB of HBM per device.

v0:
```python
import jax
import jax.numpy as jnp
from jax import lax
from jax.sharding import PartitionSpec as P

A = 8
SNPS = 16384


def solve_panel(row_values, inverse_part):
    partial_value = jnp.dot(
        inverse_part, row_values.astype(jnp.bfloat16), preferred_element_type=jnp.float32
    )
    return lax.psum(partial_value, "row")


def panel_term(panel_part, solved_bf):
    return jnp.einsum("ngc,cr->ngr", panel_part, solved_bf, preferred_element_type=jnp.float32)


def shards(residual, diag_inverse, panels, first_block, probe_solved, genotypes, annotation):
    count_blocks = residual.shape[0]
    block_now = first_block[0]
    positions = jnp.arange(count_blocks, dtype=jnp.int32)
    first_rows = lax.dynamic_index_in_dim(residual, block_now, 0, keepdims=False)
    first_solved = solve_panel(first_rows, diag_inverse[0])
    first_bf = first_solved.astype(jnp.bfloat16)
    next_panel = lax.dynamic_index_in_dim(panels[0], block_now + 1, 0, keepdims=False)
    next_sum = lax.psum(jnp.dot(next_panel, first_bf, preferred_element_type=jnp.float32), "col")
    second_rows = lax.dynamic_index_in_dim(residual, block_now + 1, 0, keepdims=False) - next_sum
    second = solve_panel(second_rows, diag_inverse[1])
    keep_first = (positions > block_now).astype(jnp.float32)[:, None, None]
    keep_second = (positions > block_now + 1).astype(jnp.float32)[:, None, None]
    summed_both = keep_first * panel_term(panels[0], first_bf) + keep_second * panel_term(
        panels[1], second.astype(jnp.bfloat16)
    )
    current = residual - lax.psum(summed_both.astype(jnp.bfloat16), "col").astype(jnp.float32)
    solved_list = [first_solved, second]
    projected = jnp.einsum(
        "ngs,ngr->sr", genotypes, probe_solved, preferred_element_type=jnp.float32
    )
    inv_snps = 1.0 / SNPS
    loadings = lax.psum(projected, "row")
    rounded = (loadings * inv_snps).astype(jnp.bfloat16)
    onehot = annotation[:, None] == jnp.arange(A, dtype=jnp.int32)[None, :]
    weights = jnp.where(onehot[:, :, None], rounded[:, None, :], jnp.zeros((), jnp.bfloat16))
    weights = weights.reshape(rounded.shape[0], A * rounded.shape[1])
    annotated = jnp.einsum("ngs,sk->ngk", genotypes, weights, preferred_element_type=jnp.float32)
    annotated = annotated.reshape(genotypes.shape[0], genotypes.shape[1], A, rounded.shape[1])
    grm_products = lax.psum_scatter(annotated, "col", scatter_dimension=2, tiled=True).astype(
        jnp.bfloat16
    )
    return (current, jnp.stack(solved_list), grm_products)


def solution(mesh):
    in_specs = (
        P(None, "row", None),
        P(None, "col", "row"),
        P(None, None, "row", "col"),
        P(),
        P(None, "row", None),
        P(None, "row", "col"),
        P("col"),
    )
    out_specs = (P(None, "row", None), P(None, "col", None), P(None, "row", "col", None))
    return jax.shard_map(shards, mesh=mesh, in_specs=in_specs, out_specs=out_specs, check_vma=False)
```

profile of v0, /device:TPU:0, one launch (start us, length us, event | category | flops | bytes accessed | tf_op | source)
XLA Modules:
  0.0 372.8 jit_solution(3764837393792807037)
XLA Ops:
  7.9 2.0 convolution_bitcast_fusion.2
  9.9 0.0 all-reduce.8.cloned.1.call-start
  10.0 9.5 %convolution_bitcast_fusion = f32[4096,128]{1,0:T(8,128)} fusion(bf16[8,256,4096]{2,1,0:T(8,128)(2,1)} %param.12, bf16[8,256,128]{2,1,0:T(8,128)(2,1)S(1)} %copy-done), kind=kOutput, calls=%fused_computation.1 | convolution fusion | flops 2147483648 | bytes 19398656 | tf_op jit(solution)/shard_map/ngs,ngr->sr/dot_general | solution.py:39
  19.5 48.8 %all-reduce.6.cloned.1.call-done = f32[512,128]{0,1:T(8,128)} async-done(((f32[512,128]{0,1:T(8,128)}), f32[512,128]{0,1:T(8,128)}) %all-reduce.6.cloned.1.call-update) | async-done | bytes 262160 | tf_op jit(solution)/shard_map/psum | solution.py:14
  68.3 1.8 fusion.21
  70.2 35.0 %all-reduce.8.cloned.1.call-done = f32[256,128]{1,0:T(8,128)} async-done(((f32[256,128]{1,0:T(8,128)}), f32[256,128]{1,0:T(8,128)}) %all-reduce.8.cloned.1.call-update) | async-done | bytes 131088 | tf_op jit(solution)/shard_map/psum | solution.py:29
  105.2 1.9 convolution_bitcast_fusion.1
  107.2 3.5 fusion.5
  110.7 61.2 %all-reduce.12.cloned.1.call-done = (f32[512,128]{0,1:T(8,128)}, f32[4096,128]{1,0:T(8,128)}) async-done(((f32[512,128]{0,1:T(8,128)}, f32[4096,128]{1,0:T(8,128)}), (f32[512,128]{0,1:T(8,128)}, f32[4096,128]{1,0:T(8,128)})) %all-reduce.12.cloned.1.call-update) | async-done | bytes 2359312 | tf_op jit(solution)/shard_map/psum | solution.py:14
  171.9 1.7 multiply_convert_fusion
  173.7 0.5 copy.18
  174.2 3.5 fusion.17
  177.8 0.6 broadcast_select_fusion
  178.4 21.9 %fusion.40 = f32[1024,8,256]{2,0,1:T(8,128)} fusion(bf16[4096,1024,1]{0,1,2:T(8,128)(2,1)S(1)} %bitcast.66, bf16[8,256,4096]{2,1,0:T(8,128)(2,1)} %param.12), kind=kOutput, calls=%fused_computation.40 | convolution fusion | flops 17179869184 | bytes 33554432 | tf_op jit(solution)/shard_map/ngs,sk->ngk/dot_general | solution.py:48
  200.3 9.2 %copy.19 = f32[8,256,8,128]{3,1,0,2:T(8,128)} copy(f32[8,256,8,128]{1,3,2,0:T(8,128)} %bitcast.67) | data formatting | bytes 16777216 | tf_op jit(solution)/shard_map/reshape | solution.py:49
  209.6 1.2 copy-done.3
  210.8 0.3 copy.16
  211.2 1.0 copy.21
  212.2 3.6 all-reduce.10.cloned.1.call-done
  215.8 1.2 convert_subtract_fusion
  217.0 1.3 copy.20
  218.3 144.1 %reduce-scatter.2.cloned.1.call-done = f32[8,256,2,128]{3,1,0,2:T(8,128)} async-done(((f32[8,256,8,128]{3,1,0,2:T(8,128)}), f32[8,256,2,128]{3,1,0,2:T(8,128)}) %reduce-scatter.2.cloned.1.call-update) | async-done | bytes 2097168 | tf_op jit(solution)/shard_map/reduce_scatter | solution.py:50
  362.4 1.8 convert_element_type.55
  364.2 2.0 copy.22
  (28 shorter events, 0.3 us)
Async XLA Ops:
  7.2 2.8 copy-start
  7.2 61.1 %all-reduce.6.cloned.1.call-start = ((), (), s32[]{:S(2)}) async-start(), calls=%async_computation.1 | async-start | bytes 524288 | tf_op jit(solution)/shard_map/psum | solution.py:14
  9.9 95.3 %all-reduce.8.cloned.1.call-start = ((), (), s32[]{:S(2)}) async-start(), calls=%async_computation.2 | async-start | bytes 262144 | tf_op jit(solution)/shard_map/psum | solution.py:29
  19.5 48.8 %slice-start = ((bf16[2,8,256,512]{3,2,1,0:T(8,128)(2,1)}), bf16[1,8,256,512]{3,2,1,0:T(8,128)(2,1)S(1)}, s32[]{:S(2)}) async-start(bf16[2,8,256,512]{3,2,1,0:T(8,128)(2,1)} %param.9), calls=%async_computation.6 | async-start | bytes 4194304 | tf_op jit(solution)/shard_map/slice | solution.py:34
  19.5 85.8 %copy-start.5 = (bf16[2,512,256]{2,1,0:T(8,128)(2,1)S(1)}, bf16[2,512,256]{2,1,0:T(8,128)(2,1)}, u32[]{:S(2)}) copy-start(bf16[2,512,256]{2,1,0:T(8,128)(2,1)} %param.8) | copy-start | bytes 1572868
  19.5 87.7 %copy-start.6 = (s32[4096]{0:T(1024)S(1)}, s32[4096]{0:T(1024)}, u32[]{:S(2)}) copy-start(s32[4096]{0:T(1024)} %param.13) | copy-start | bytes 49156
  70.1 101.8 %all-reduce.12.cloned.1.call-start = ((), (), s32[]{:S(2)}) async-start(), calls=%async_computation.5 | async-start | bytes 4718592 | tf_op jit(solution)/shard_map/psum | solution.py:14
  107.2 108.6 %all-reduce.10.cloned.1.call-start = ((), (), s32[]{:S(2)}) async-start(), calls=%async_computation.3 | async-start | bytes 1048576 | tf_op jit(solution)/shard_map/psum | solution.py:37
  171.9 2.3 copy-start.4
  177.7 184.7 %reduce-scatter.2.cloned.1.call-start = ((), (), s32[]{:S(2)}) async-start(), calls=%async_computation.4 | async-start | bytes 10485760 | tf_op jit(solution)/shard_map/reduce_scatter | solution.py:50
  209.5 1.2 copy-start.3
  209.5 1.6 copy-start.2
  215.8 150.5 %copy-start.1 = (bf16[8,256,128]{2,1,0:T(8,128)(2,1)S(1)}, bf16[8,256,128]{2,1,0:T(8,128)(2,1)}, u32[]{:S(2)}) copy-start(bf16[8,256,128]{2,1,0:T(8,128)(2,1)} %param.11) | copy-start | bytes 1572868
Sparse Core Ops, SparseCore 0:
  11.6 56.5 all-reduce.5
  71.1 34.0 all-reduce.7
  109.2 62.7 all-reduce.11
  177.8 37.8 all-reduce.9
  218.0 144.4 reduce-scatter.1
where the time goes:
time: 373 us
  waiting for transfers between devices  293 us (79%)
  matrix products  44.1 us (12%)
  local copies, waits for them, and re-layouts  15.6 us (4%)
  between operations  14.6 us (4%)
  other arithmetic  5.44 us (1%)
    reduce_scatter x1, waiting for transfers between devices, shards(): lax.psum_scatter(annotated, 'col', scatter_dimension=2, tiled=True)  144 us
    psum x2, waiting for transfers between devices, solve_panel(): return lax.psum(partial_value, 'row')  110 us
    psum x1, waiting for transfers between devices, shards(): lax.psum(jnp.dot(next_panel, first_bf, preferred_element_type=jnp.float32...  35 us
    dot_general x1, matrix products, shards(): jnp.einsum('ngs,sk->ngk', genotypes, weights, preferred_element_type=jnp....  21.9 us
    dot_general x1, matrix products, shards(): jnp.einsum('ngs,ngr->sr', genotypes, probe_solved, preferred_element_type...  9.5 us
    reshape x1, local copies, waits for them, and re-layouts, shards(): annotated.reshape(genotypes.shape[0], genotypes.shape[1], A, rounded.shap...  9.2 us
  transfers between devices with their start and end apart: 5, of which 5 were waited for; matrix products, arithmetic and copies ran while one was open for 13% of the time, Pallas kernels for 0%

commit v1 on v0

v1 whole, which is shorter than its diff:
```python
import jax
import jax.numpy as jnp
from jax import lax
from jax.experimental import pallas as pl
from jax.experimental.pallas import tpu as pltpu
from jax.sharding import PartitionSpec as P

A = 8
BF = jnp.bfloat16
F32 = jnp.float32


def project_kernel(core_ref, probe_ref, geno_ref, *rest):
    outs, turned = rest[:-1], rest[-1]

    @pl.when(pl.program_id(0) == 0)
    def _():
        turned[...] = probe_ref[...].T

    acc = jnp.dot(turned[...], geno_ref[...], preferred_element_type=F32)
    core = core_ref[0]
    half = acc.shape[0] // 2
    quarter = half // 2
    for h in range(2):
        low = acc[h * half : h * half + quarter]
        high = acc[h * half + quarter : (h + 1) * half]
        outs[2 * h][...] = jnp.where(core == 0, low, high)
        outs[2 * h + 1][...] = jnp.where(core == 0, high, low).astype(BF)


def project(core, probe, geno):
    rows, snps = geno.shape
    rhs = probe.shape[1]
    tile = min(512, snps)
    quarter = rhs // 4
    out_spec = pl.BlockSpec((quarter, tile), lambda i, c: (0, i))
    shapes = []
    for _ in range(2):
        shapes += [jax.ShapeDtypeStruct((quarter, snps), F32), jax.ShapeDtypeStruct((quarter, snps), BF)]
    return pl.pallas_call(
        project_kernel,
        grid_spec=pltpu.PrefetchScalarGridSpec(
            num_scalar_prefetch=1,
            grid=(snps // tile,),
            in_specs=[
                pl.BlockSpec((rows, rhs), lambda i, c: (0, 0)),
                pl.BlockSpec((rows, tile), lambda i, c: (0, i)),
            ],
            out_specs=[out_spec] * 4,
            scratch_shapes=[pltpu.VMEM((rhs, rows), BF)],
        ),
        out_shape=shapes,
        name="project",
    )(core, probe, geno)


def annotate_kernel(slices, per_slice, ids_ref, load_ref, ann_ref, geno_ref, *rest):
    outs, weights = rest[:-1], rest[-1]
    width = load_ref.shape[0]

    @pl.when(pl.program_id(0) == 0)
    def _():
        for s in range(slices):
            for a in range(per_slice):
                mask = (ann_ref[...] == ids_ref[s] * per_slice + a).astype(F32).astype(BF)
                spot = (s * per_slice + a) * width
                weights[spot : spot + width, :] = load_ref[...] * mask

    acc = lax.dot_general(
        geno_ref[...], weights[...], (((1,), (1,)), ((), ())), preferred_element_type=F32
    )
    wide = per_slice * width
    for s in range(slices):
        outs[s][...] = acc[:, s * wide : (s + 1) * wide].astype(BF)


def annotate(ids, load, ann, geno, per_slice):
    rows, snps = geno.shape
    slices = ids.shape[0]
    width = load.shape[0]
    tile = min(256, rows)
    wide = per_slice * width

    def kernel(*refs):
        annotate_kernel(slices, per_slice, *refs)

    return pl.pallas_call(
        kernel,
        grid_spec=pltpu.PrefetchScalarGridSpec(
            num_scalar_prefetch=1,
            grid=(rows // tile,),
            in_specs=[
                pl.BlockSpec((width, snps), lambda i, c: (0, 0)),
                pl.BlockSpec((1, snps), lambda i, c: (0, 0)),
                pl.BlockSpec((tile, snps), lambda i, c: (i, 0)),
            ],
            out_specs=[pl.BlockSpec((tile, wide), lambda i, c: (i, 0))] * slices,
            scratch_shapes=[pltpu.VMEM((slices * wide, snps), BF)],
        ),
        out_shape=[jax.ShapeDtypeStruct((rows, wide), BF)] * slices,
        name="annotate",
    )(ids, load, ann, geno)


def flip(x, axis, size, bits):
    return lax.ppermute(x, axis, [(i, i ^ bits) for i in range(size)])


def pick(index, table, choose):
    distinct = sorted(set(table))
    out = choose(distinct[0])
    for p in distinct[1:]:
        here = False
        for i, q in enumerate(table):
            if q == p:
                here = here | (index == i)
        out = jnp.where(here, choose(p), out)
    return out


def make_shards(nr, nc):
    chips = nr // 2

    def row_sum(x, core):
        half = x.shape[0] // 2
        low, high = x[:half], x[half:]
        mine = jnp.where(core == 0, low, high)
        other = jnp.where(core == 0, high, low).astype(BF)
        mine = mine + flip(other, "row", nr, 1).astype(F32)
        sent = mine.astype(BF)
        for q in range(1, chips):
            mine = mine + flip(sent, "row", nr, 2 * q).astype(F32)
        other = flip(mine, "row", nr, 1)
        return jnp.concatenate(
            [jnp.where(core == 0, mine, other), jnp.where(core == 0, other, mine)], axis=0
        )

    def col_sum_small(x):
        sent = x.astype(BF)
        for q in range(1, nc):
            x = x + flip(sent, "col", nc, q).astype(F32)
        return x

    def col_sum_large(x, col):
        bits = []
        b = 1
        while b < nc:
            bits.append(b)
            b *= 2
        for b in bits:
            half = x.shape[0] // 2
            up = (col & b) != 0
            mine = jnp.where(up, x[half:], x[:half])
            other = jnp.where(up, x[:half], x[half:])
            x = (mine.astype(F32) + flip(other, "col", nc, b).astype(F32)).astype(BF)
        for b in reversed(bits):
            up = (col & b) != 0
            other = flip(x, "col", nc, b)
            x = jnp.concatenate([jnp.where(up, other, x), jnp.where(up, x, other)], axis=0)
        return x

    def loadings_half(keep, sent, core, row, scale):
        chip = row // 2
        mine = keep + flip(sent, "row", nr, 1).astype(F32)
        part = mine.shape[0] // chips
        parts = mine.reshape(chips, part, mine.shape[1])
        total = lax.dynamic_index_in_dim(parts, chip, 0, keepdims=False)
        for q in range(1, chips):
            piece = lax.dynamic_index_in_dim(parts, chip ^ q, 0, keepdims=False).astype(BF)
            total = total + flip(piece, "row", nr, 2 * q).astype(F32)
        total = (total * scale).astype(BF)
        got = [total] + [flip(total, "row", nr, 2 * q) for q in range(1, chips)]
        tables = [[c ^ q for c in range(chips)] for q in range(chips)]
        mine = jnp.concatenate([pick(chip, t, lambda p: got[p]) for t in tables], axis=0)
        other = flip(mine, "row", nr, 1)
        return jnp.concatenate(
            [jnp.where(core == 0, mine, other), jnp.where(core == 0, other, mine)], axis=0
        )

    def line_scatter(own, col):
        near = nc // 2

        def position(z, s):
            return nc - 1 - s if z < near else s

        def right_table(t):
            return [position(z, nc - 1 - t + z) if z <= t else None for z in range(nc)]

        def left_table(t):
            return [position(z, t - (nc - 1 - z)) if nc - 1 - z <= t else None for z in range(nc)]

        def filled(table):
            some = [p for p in table if p is not None][0]
            return [some if p is None else p for p in table]

        from_left = from_right = None
        for t in range(nc - 1):
            right = [(z, z + 1) for z in range(nc) if z <= t]
            left = [(z, z - 1) for z in range(nc) if nc - 1 - z <= t]
            send_right = pick(col, filled(right_table(t)), lambda p: own[p])
            send_left = pick(col, filled(left_table(t)), lambda p: own[p])
            if t > 0:
                send_right = (send_right.astype(F32) + from_left.astype(F32)).astype(BF)
                send_left = (send_left.astype(F32) + from_right.astype(F32)).astype(BF)
            from_left = lax.ppermute(send_right, "col", right)
            from_right = lax.ppermute(send_left, "col", left)
        last = pick(col, [position(z, z) for z in range(nc)], lambda p: own[p])
        return last.astype(F32) + from_left.astype(F32) + from_right.astype(F32)

    def shards(residual, diag_inverse, panels, first_block, probe_solved, genotypes, annotation):
        nblk, g, rhs = residual.shape
        row = lax.axis_index("row")
        col = lax.axis_index("col")
        core = row % 2
        scale = 1.0 / (annotation.shape[0] * nc)
        geno = genotypes.reshape(-1, genotypes.shape[2])
        probe = probe_solved.reshape(-1, rhs)
        block_now = first_block[0]

        pieces = project(core[None].astype(jnp.int32), probe, geno)

        first_rows = lax.dynamic_index_in_dim(residual, block_now, 0, keepdims=False)
        first = row_sum(jnp.dot(diag_inverse[0], first_rows.astype(BF), preferred_element_type=F32), core)
        first_bf = first.astype(BF)

        ann = annotation.reshape(1, -1)
        per_slice = A // nc
        near = col < nc // 2
        order = [jnp.where(near, nc - 1 - p, p) for p in range(nc)]
        summed = []
        for h in range(2):
            load = loadings_half(pieces[2 * h], pieces[2 * h + 1], core, row, scale)
            own = []
            for p in range(0, nc, 2):
                ids = jnp.stack(order[p : p + 2]).astype(jnp.int32)
                own += annotate(ids, load, ann, geno, per_slice)
            summed.append(line_scatter(own, col))

        next_panel = lax.dynamic_index_in_dim(panels[0], block_now + 1, 0, keepdims=False)
        next_sum = col_sum_small(jnp.dot(next_panel, first_bf, preferred_element_type=F32))
        second_rows = lax.dynamic_index_in_dim(residual, block_now + 1, 0, keepdims=False) - next_sum
        second = row_sum(
            jnp.dot(diag_inverse[1], second_rows.astype(BF), preferred_element_type=F32), core
        )
        second_bf = second.astype(BF)
        late = jnp.arange(2, nblk, dtype=jnp.int32)
        keep_first = (late > block_now).astype(F32)[:, None, None]
        keep_second = (late > block_now + 1).astype(F32)[:, None, None]
        both = keep_first * jnp.einsum(
            "ngc,cr->ngr", panels[0, 2:], first_bf, preferred_element_type=F32
        ) + keep_second * jnp.einsum(
            "ngc,cr->ngr", panels[1, 2:], second_bf, preferred_element_type=F32
        )
        update = col_sum_large(both.astype(BF).reshape(-1, rhs), col).reshape(nblk - 2, g, rhs)
        current = jnp.concatenate([residual[:2], residual[2:] - update.astype(F32)], axis=0)
        spot = jnp.arange(nblk, dtype=jnp.int32)[:, None, None] == block_now + 1
        current = jnp.where(spot, second_rows[None], current)

        half = rhs // 2
        products = jnp.stack(summed, axis=1)
        products = products.reshape(nblk, g, 2, per_slice, half)
        products = jnp.swapaxes(products, 2, 3).reshape(nblk, g, per_slice, rhs).astype(BF)
        return current, jnp.stack([first, second]), products

    return shards


def solution(mesh):
    in_specs = (
        P(None, "row", None),
        P(None, "col", "row"),
        P(None, None, "row", "col"),
        P(),
        P(None, "row", None),
        P(None, "row", "col"),
        P("col"),
    )
    out_specs = (P(None, "row", None), P(None, "col", None), P(None, "row", "col", None))
    shards = make_shards(mesh.shape["row"], mesh.shape["col"])
    return jax.shard_map(shards, mesh=mesh, in_specs=in_specs, out_specs=out_specs, check_vma=False)
```

time: 373 us -> 196 us (0.53)
  waiting for transfers between devices: 293 us -> 38.8 us
  starting transfers between devices: 0.21 us -> 68.6 us
  Pallas kernels: 0 us -> 60.2 us
  matrix products: 44.1 us -> 1.98 us
  between operations: 14.6 us -> 2.06 us
  local copies, waits for them, and re-layouts: 15.6 us -> 4.99 us
  other arithmetic: 5.44 us -> 15.7 us
    psum x4 -> x0, waiting for transfers between devices: 149 us -> none  [the longest x2 110 us: solve_panel(): return lax.psum(partial_value, 'row')]
    reduce_scatter x1 -> x0, waiting for transfers between devices: 144 us -> none  [shards(): lax.psum_scatter(annotated, 'col', scatter_dimension=2, tiled=True)]
    ppermute x0 -> x45, starting transfers between devices: none -> 68.6 us  [the longest x33 32.8 us: flip(): return lax.ppermute(x, axis, [(i, i ^ bits) for i in range(size)])]
    pallas_call x0 -> x5, Pallas kernels: none -> 60.2 us  [the longest x4 49.5 us: annotate(): pl.pallas_call(kernel, grid_spec=pltpu.PrefetchScalarGridSpec(num_scalar_...]
    dot_general x7 -> x5, matrix products: 44.1 us -> 1.98 us  [the longest x1 0.65 us: shards(): jnp.einsum('ngc,cr->ngr', panels[1, 2:], second_bf, preferred_element_typ...]
    ppermute x0 -> x45, waiting for transfers between devices: none -> 38.8 us  [the longest x33 23.1 us: flip(): return lax.ppermute(x, axis, [(i, i ^ bits) for i in range(size)])]
    reshape x1 -> x0, local copies, waits for them, and re-layouts: 9.2 us -> none  [shards(): annotated.reshape(genotypes.shape[0], genotypes.shape[1], A, rounded.shap...]
    select_n x1 -> x11, other arithmetic: 0.64 us -> 4.39 us  [the longest x2 2.08 us: loadings_half(): jnp.where(core == 0, mine, other)]
  transfers between devices with their start and end apart: 5 -> 45, of which waited for: 5 -> 18; matrix products, arithmetic and copies ran while one was open for 13% -> 10% of each run, Pallas kernels for 0% -> 26%
where the time goes in v1:
time: 196 us; the launch traced here: 192 us
  starting transfers between devices  68.6 us (35%)
  Pallas kernels  60.2 us (31%)
  waiting for transfers between devices  38.8 us (20%)
  other arithmetic  15.7 us (8%)
  local copies, waits for them, and re-layouts  4.99 us (3%)
  between operations  2.06 us (1%)
  matrix products  1.98 us (1%)
    pallas_call x4, Pallas kernels, annotate(): pl.pallas_call(kernel, grid_spec=pltpu.PrefetchScalarGridSpec(num_scalar_...  49.5 us
    ppermute x33, starting transfers between devices, flip(): return lax.ppermute(x, axis, [(i, i ^ bits) for i in range(size)])  32.8 us
    ppermute x6, starting transfers between devices, line_scatter(): from_left = lax.ppermute(send_right, 'col', right)  28.7 us
    ppermute x33, waiting for transfers between devices, flip(): return lax.ppermute(x, axis, [(i, i ^ bits) for i in range(size)])  23.1 us
    ppermute x6, waiting for transfers between devices, line_scatter(): from_left = lax.ppermute(send_right, 'col', right)  15.6 us
    pallas_call x1, Pallas kernels, project(): pl.pallas_call(project_kernel, grid_spec=pltpu.PrefetchScalarGridSpec(num...  10.6 us
    ppermute x6, starting transfers between devices, line_scatter(): from_right = lax.ppermute(send_left, 'col', left)  7.06 us
    convert_element_type x4, other arithmetic, line_scatter(): send_right = (send_right.astype(F32) + from_left.astype(F32)).astype(BF)  3.99 us
  transfers between devices with their start and end apart: 45, of which 18 were waited for; matrix products, arithmetic and copies ran while one was open for 10% of the time, Pallas kernels for 26%

profile of v1, /device:TPU:0, one launch (start us, length us, event | category | flops | bytes accessed | tf_op | source)
XLA Modules:
  0.0 192.3 jit_solution(12523090319654192561)
XLA Ops:
  0.7 10.6 %project.1 = (f32[32,4096]{1,0:T(8,128)}, bf16[32,4096]{1,0:T(8,128)(2,1)}, f32[32,4096]{1,0:T(8,128)}, bf16[32,4096]{1,0:T(8,128)(2,1)}) custom-call(s32[1]{0:T(128)} %bitcast.20.core_ref, bf16[2048,128]{1,0:T(8,128)(2,1)} %bitcast.130, bf16[2048,4096]{1,0:T(8,128)(2,1)} %bitcast.119), custom_call_target="tpu_custom_call" | custom-call | tf_op jit(solution)/shard_map/project/pallas_call | solution.py:40
  14.2 2.9 %collective-permute-start.1 = (bf16[256,128]{0,1:T(8,128)(2,1)S(1)}, bf16[256,128]{0,1:T(8,128)(2,1)S(1)}, u32[]{:S(2)}, u32[]{:S(2)}) collective-permute-start(bf16[256,128]{0,1:T(8,128)(2,1)S(1)} %fusion.57), channel_id=1, source_target_pairs={{0,8},{4,12},{8,0},{12,4},{16,24},{20,28},{24,16},{28,20},{1,9},{5... | collective-permute-start | bytes 196616 | tf_op jit(solution)/shard_map/ppermute | solution.py:106
  19.5 1.9 collective-permute-done.2
  21.4 2.4 %collective-permute-done.3 = bf16[256,128]{0,1:T(8,128)(2,1)S(1)} collective-permute-done((bf16[256,128]{0,1:T(8,128)(2,1)S(1)}, bf16[256,128]{0,1:T(8,128)(2,1)S(1)}, u32[]{:S(2)}, u32[]{:S(2)}) %collective-permute-start.3) | collective-permute-done | bytes 65568 | tf_op jit(solution)/shard_map/ppermute | solution.py:106
  28.2 2.6 %collective-permute-start.6 = (bf16[256,128]{1,0:T(8,128)(2,1)S(1)}, bf16[256,128]{1,0:T(8,128)(2,1)S(1)}, u32[]{:S(2)}, u32[]{:S(2)}) collective-permute-start(bf16[256,128]{1,0:T(8,128)(2,1)S(1)} %get-tuple-element.69), channel_id=1, source_target_pairs={{0,2},{1,3},{2,0},{3,1},{4,6},{5,7},{6,4},{7,5},{8,10},{9,11},{10,... | collective-permute-start | bytes 196616 | tf_op jit(solution)/shard_map/ppermute | solution.py:106
  33.1 2.4 %collective-permute-start.20 = (bf16[8,4096]{1,0:T(8,128)(2,1)S(1)}, bf16[8,4096]{1,0:T(8,128)(2,1)S(1)}, u32[]{:S(2)}, u32[]{:S(2)}) collective-permute-start(bf16[8,4096]{1,0:T(8,128)(2,1)S(1)} %get-tuple-element.44), channel_id=1, source_target_pairs={{0,24},{4,28},{8,16},{12,20},{16,8},{20,12},{24,0},{28,4},{1,25},{... | collective-permute-start | bytes 196616 | tf_op jit(solution)/shard_map/ppermute | solution.py:106
  41.8 1.7 collective-permute-start.21
  54.8 1.7 collective-permute-done.11
  64.5 12.4 %annotate.5 = (bf16[2048,128]{1,0:T(8,128)(2,1)}, bf16[2048,128]{1,0:T(8,128)(2,1)}) custom-call(s32[2]{0:T(128)} %get-tuple-element.72.refs_0_, bf16[64,4096]{1,0:T(8,128)(2,1)} %pad_maximum_fusion.1.refs_1_, s32[1,4096]{1,0:T(1,128)} %bitcast.131, bf16[2048,4096]{1,0:T(8,128)(2,1)} %bitcast.120), custom_call_target="tpu_custom_call" | custom-call | tf_op jit(solution)/shard_map/annotate/pallas_call | solution.py:87
  76.9 3.5 %collective-permute-start.25 = (bf16[2048,128]{1,0:T(8,128)(2,1)}, bf16[2048,128]{1,0:T(8,128)(2,1)S(1)}, u32[]{:S(2)}, u32[]{:S(2)}) collective-permute-start(bf16[2048,128]{1,0:T(8,128)(2,1)} %get-tuple-element.20), channel_id=1, source_target_pairs={{0,1},{4,5},{8,9},{12,13},{16,17},{20,21},{24,25},{28,29}} | collective-permute-start | bytes 1572872 | tf_op jit(solution)/shard_map/ppermute | solution.py:205
  83.0 10.8 %collective-permute-done.14 = bf16[384,128]{1,0:T(8,128)(2,1)S(1)} collective-permute-done((bf16[384,128]{1,0:T(8,128)(2,1)S(1)}, bf16[384,128]{1,0:T(8,128)(2,1)S(1)}, u32[]{:S(2)}, u32[]{:S(2)}) %collective-permute-start.14) | collective-permute-done | bytes 98336 | tf_op jit(solution)/shard_map/ppermute | solution.py:106
  93.9 3.4 %collective-permute-start.15 = (bf16[384,128]{1,0:T(8,128)(2,1)S(1)}, bf16[384,128]{1,0:T(8,128)(2,1)S(1)}, u32[]{:S(2)}, u32[]{:S(2)}) collective-permute-start(bf16[384,128]{1,0:T(8,128)(2,1)S(1)} %add_convert_fusion.10), channel_id=1, source_target_pairs={{0,2},{1,3},{2,0},{3,1},{4,6},{5,7},{6,4},{7,5},{8,10},{9,11},{10,... | collective-permute-start | bytes 294920 | tf_op jit(solution)/shard_map/ppermute | solution.py:106
  98.2 12.3 %annotate.7 = (bf16[2048,128]{1,0:T(8,128)(2,1)}, bf16[2048,128]{1,0:T(8,128)(2,1)}) custom-call(s32[2]{0:T(128)} %get-tuple-element.72.refs_0_, bf16[64,4096]{1,0:T(8,128)(2,1)} %pad_maximum_fusion.2.refs_1_, s32[1,4096]{1,0:T(1,128)} %bitcast.132, bf16[2048,4096]{1,0:T(8,128)(2,1)} %bitcast.121), custom_call_target="tpu_custom_call" | custom-call | tf_op jit(solution)/shard_map/annotate/pallas_call | solution.py:87
  110.5 2.6 %collective-permute-start.39 = (bf16[2048,128]{1,0:T(8,128)(2,1)}, bf16[2048,128]{1,0:T(8,128)(2,1)}, u32[]{:S(2)}, u32[]{:S(2)}) collective-permute-start(bf16[2048,128]{1,0:T(8,128)(2,1)} %get-tuple-element.26), channel_id=1, source_target_pairs={{0,1},{4,5},{8,9},{12,13},{16,17},{20,21},{24,25},{28,29}} | collective-permute-start | bytes 1572872 | tf_op jit(solution)/shard_map/ppermute | solution.py:205
  114.6 12.4 %annotate.4 = (bf16[2048,128]{1,0:T(8,128)(2,1)}, bf16[2048,128]{1,0:T(8,128)(2,1)}) custom-call(s32[2]{0:T(128)} %get-tuple-element.71.refs_0_, bf16[64,4096]{1,0:T(8,128)(2,1)} %pad_maximum_fusion.1.refs_1_, s32[1,4096]{1,0:T(1,128)} %bitcast.133, bf16[2048,4096]{1,0:T(8,128)(2,1)} %bitcast.122), custom_call_target="tpu_custom_call" | custom-call | tf_op jit(solution)/shard_map/annotate/pallas_call | solution.py:87
  126.9 12.5 %annotate.6 = (bf16[2048,128]{1,0:T(8,128)(2,1)}, bf16[2048,128]{1,0:T(8,128)(2,1)}) custom-call(s32[2]{0:T(128)} %get-tuple-element.71.refs_0_, bf16[64,4096]{1,0:T(8,128)(2,1)} %pad_maximum_fusion.2.refs_1_, s32[1,4096]{1,0:T(1,128)} %bitcast.134, bf16[2048,4096]{1,0:T(8,128)(2,1)} %bitcast.123), custom_call_target="tpu_custom_call" | custom-call | tf_op jit(solution)/shard_map/annotate/pallas_call | solution.py:87
  141.1 3.8 %collective-permute-start.26 = (bf16[2048,128]{1,0:T(8,128)(2,1)S(1)}, bf16[2048,128]{1,0:T(8,128)(2,1)S(1)}, u32[]{:S(2)}, u32[]{:S(2)}) collective-permute-start(bf16[2048,128]{1,0:T(8,128)(2,1)S(1)} %get-tuple-element.37), channel_id=1, source_target_pairs={{0,1},{1,2},{4,5},{5,6},{8,9},{9,10},{12,13},{13,14},{16,17},{17,1... | collective-permute-start | bytes 1572872 | tf_op jit(solution)/shard_map/ppermute | solution.py:205
  147.3 3.5 %collective-permute-start.40 = (bf16[2048,128]{1,0:T(8,128)(2,1)S(1)}, bf16[2048,128]{1,0:T(8,128)(2,1)S(1)}, u32[]{:S(2)}, u32[]{:S(2)}) collective-permute-start(bf16[2048,128]{1,0:T(8,128)(2,1)S(1)} %get-tuple-element.39), channel_id=1, source_target_pairs={{0,1},{1,2},{4,5},{5,6},{8,9},{9,10},{12,13},{13,14},{16,17},{17,1... | collective-permute-start | bytes 1572872 | tf_op jit(solution)/shard_map/ppermute | solution.py:205
  151.8 5.5 %collective-permute-done.26 = bf16[2048,128]{1,0:T(8,128)(2,1)S(1)} collective-permute-done((bf16[2048,128]{1,0:T(8,128)(2,1)S(1)}, bf16[2048,128]{1,0:T(8,128)(2,1)S(1)}, u32[]{:S(2)}, u32[]{:S(2)}) %collective-permute-start.26) | collective-permute-done | bytes 524320 | tf_op jit(solution)/shard_map/ppermute | solution.py:205
  157.7 7.3 %collective-permute-start.27 = (bf16[2048,128]{1,0:T(8,128)(2,1)S(1)}, bf16[2048,128]{1,0:T(8,128)(2,1)S(1)}, u32[]{:S(2)}, u32[]{:S(2)}) collective-permute-start(bf16[2048,128]{1,0:T(8,128)(2,1)S(1)} %get-tuple-element.33), channel_id=1, source_target_pairs={{0,1},{1,2},{2,3},{4,5},{5,6},{6,7},{8,9},{9,10},{10,11},{12,13},{... | collective-permute-start | bytes 1572872 | tf_op jit(solution)/shard_map/ppermute | solution.py:205
  166.5 2.0 %collective-permute-done.40 = bf16[2048,128]{1,0:T(8,128)(2,1)S(1)} collective-permute-done((bf16[2048,128]{1,0:T(8,128)(2,1)S(1)}, bf16[2048,128]{1,0:T(8,128)(2,1)S(1)}, u32[]{:S(2)}, u32[]{:S(2)}) %collective-permute-start.40) | collective-permute-done | bytes 524320 | tf_op jit(solution)/shard_map/ppermute | solution.py:205
  168.9 8.0 %collective-permute-start.41 = (bf16[2048,128]{1,0:T(8,128)(2,1)S(1)}, bf16[2048,128]{1,0:T(8,128)(2,1)}, u32[]{:S(2)}, u32[]{:S(2)}) collective-permute-start(bf16[2048,128]{1,0:T(8,128)(2,1)S(1)} %get-tuple-element.35), channel_id=1, source_target_pairs={{0,1},{1,2},{2,3},{4,5},{5,6},{6,7},{8,9},{9,10},{10,11},{12,13},{... | collective-permute-start | bytes 1572872 | tf_op jit(solution)/shard_map/ppermute | solution.py:205
  180.3 7.8 %collective-permute-done.41 = bf16[2048,128]{1,0:T(8,128)(2,1)} collective-permute-done((bf16[2048,128]{1,0:T(8,128)(2,1)S(1)}, bf16[2048,128]{1,0:T(8,128)(2,1)}, u32[]{:S(2)}, u32[]{:S(2)}) %collective-permute-start.41) | collective-permute-done | bytes 524320 | tf_op jit(solution)/shard_map/ppermute | solution.py:205
  190.3 2.0 %copy.18 = bf16[8,256,2,128]{3,2,1,0:T(2,128)(2,1)} copy(bf16[8,256,2,128]{1,3,2,0:T(8,128)(2,1)S(1)} %bitcast.124) | data formatting | bytes 2097152
  (162 shorter events, 54.3 us)
Async XLA Ops:
  11.3 19.5 %collective-permute-start.17 = (bf16[32,4096]{1,0:T(8,128)(2,1)}, bf16[32,4096]{1,0:T(8,128)(2,1)}, u32[]{:S(2)}, u32[]{:S(2)}) collective-permute-start(bf16[32,4096]{1,0:T(8,128)(2,1)} %get-tuple-element.16), channel_id=1, source_target_pairs={{0,4},{4,0},{8,12},{12,8},{16,20},{20,16},{24,28},{28,24},{1,5},{5... | collective-permute-start | bytes 786440 | tf_op jit(solution)/shard_map/ppermute | solution.py:106
  11.8 21.3 %collective-permute-start.31 = (bf16[32,4096]{1,0:T(8,128)(2,1)}, bf16[32,4096]{1,0:T(8,128)(2,1)S(1)}, u32[]{:S(2)}, u32[]{:S(2)}) collective-permute-start(bf16[32,4096]{1,0:T(8,128)(2,1)} %get-tuple-element.22), channel_id=1, source_target_pairs={{0,4},{4,0},{8,12},{12,8},{16,20},{20,16},{24,28},{28,24},{1,5},{5... | collective-permute-start | bytes 786440 | tf_op jit(solution)/shard_map/ppermute | solution.py:106
  26.6 13.9 %collective-permute-start.5 = (bf16[256,128]{1,0:T(8,128)(2,1)S(1)}, bf16[256,128]{1,0:T(8,128)(2,1)S(1)}, u32[]{:S(2)}, u32[]{:S(2)}) collective-permute-start(bf16[256,128]{1,0:T(8,128)(2,1)S(1)} %get-tuple-element.69), channel_id=1, source_target_pairs={{0,1},{1,0},{2,3},{3,2},{4,5},{5,4},{6,7},{7,6},{8,9},{9,8},{10,11... | collective-permute-start | bytes 196616 | tf_op jit(solution)/shard_map/ppermute | solution.py:106
  28.2 13.6 %collective-permute-start.6 = (bf16[256,128]{1,0:T(8,128)(2,1)S(1)}, bf16[256,128]{1,0:T(8,128)(2,1)S(1)}, u32[]{:S(2)}, u32[]{:S(2)}) collective-permute-start(bf16[256,128]{1,0:T(8,128)(2,1)S(1)} %get-tuple-element.69), channel_id=1, source_target_pairs={{0,2},{1,3},{2,0},{3,1},{4,6},{5,7},{6,4},{7,5},{8,10},{9,11},{10,... | collective-permute-start | bytes 196616 | tf_op jit(solution)/shard_map/ppermute | solution.py:106
  37.3 7.0 %collective-permute-start.32 = (bf16[8,4096]{1,0:T(8,128)(2,1)S(1)}, bf16[8,4096]{1,0:T(8,128)(2,1)S(1)}, u32[]{:S(2)}, u32[]{:S(2)}) collective-permute-start(bf16[8,4096]{1,0:T(8,128)(2,1)S(1)} %get-tuple-element.48), channel_id=1, source_target_pairs={{0,8},{4,12},{8,0},{12,4},{16,24},{20,28},{24,16},{28,20},{1,9},{5... | collective-permute-start | bytes 196616 | tf_op jit(solution)/shard_map/ppermute | solution.py:106
  41.8 6.9 %collective-permute-start.21 = (bf16[8,4096]{1,0:T(8,128)(2,1)S(1)}, bf16[8,4096]{1,0:T(8,128)(2,1)S(1)}, u32[]{:S(2)}, u32[]{:S(2)}) collective-permute-start(bf16[8,4096]{1,0:T(8,128)(2,1)S(1)} %fusion.42), channel_id=1, source_target_pairs={{0,24},{4,28},{8,16},{12,20},{16,8},{20,12},{24,0},{28,4},{1,25},{... | collective-permute-start | bytes 196616 | tf_op jit(solution)/shard_map/ppermute | solution.py:106
  54.1 8.5 %collective-permute-start.24 = (bf16[32,4096]{1,0:T(8,128)(2,1)}, bf16[32,4096]{1,0:T(8,128)(2,1)}, u32[]{:S(2)}, u32[]{:S(2)}) collective-permute-start(bf16[32,4096]{1,0:T(8,128)(2,1)} %pad_maximum_fusion.6), channel_id=1, source_target_pairs={{0,4},{4,0},{8,12},{12,8},{16,20},{20,16},{24,28},{28,24},{1,5},{5... | collective-permute-start | bytes 786440 | tf_op jit(solution)/shard_map/ppermute | solution.py:106
  58.1 23.9 %collective-permute-start.38 = (bf16[32,4096]{1,0:T(8,128)(2,1)}, bf16[32,4096]{1,0:T(8,128)(2,1)}, u32[]{:S(2)}, u32[]{:S(2)}) collective-permute-start(bf16[32,4096]{1,0:T(8,128)(2,1)} %pad_maximum_fusion.7), channel_id=1, source_target_pairs={{0,4},{4,0},{8,12},{12,8},{16,20},{20,16},{24,28},{28,24},{1,5},{5... | collective-permute-start | bytes 786440 | tf_op jit(solution)/shard_map/ppermute | solution.py:106
  62.0 19.8 %collective-permute-start.13 = (bf16[768,128]{1,0:T(8,128)(2,1)}, bf16[768,128]{1,0:T(8,128)(2,1)S(1)}, u32[]{:S(2)}, u32[]{:S(2)}) collective-permute-start(bf16[768,128]{1,0:T(8,128)(2,1)} %bitcast.14), channel_id=1, source_target_pairs={{0,1},{1,0},{2,3},{3,2},{4,5},{5,4},{6,7},{7,6},{8,9},{9,8},{10,11... | collective-permute-start | bytes 589832 | tf_op jit(solution)/shard_map/ppermute | solution.py:106
  76.9 62.7 %collective-permute-start.25 = (bf16[2048,128]{1,0:T(8,128)(2,1)}, bf16[2048,128]{1,0:T(8,128)(2,1)S(1)}, u32[]{:S(2)}, u32[]{:S(2)}) collective-permute-start(bf16[2048,128]{1,0:T(8,128)(2,1)} %get-tuple-element.20), channel_id=1, source_target_pairs={{0,1},{4,5},{8,9},{12,13},{16,17},{20,21},{24,25},{28,29}} | collective-permute-start | bytes 1572872 | tf_op jit(solution)/shard_map/ppermute | solution.py:205
  80.4 59.2 %collective-permute-start.28 = (bf16[2048,128]{1,0:T(8,128)(2,1)}, bf16[2048,128]{1,0:T(8,128)(2,1)}, u32[]{:S(2)}, u32[]{:S(2)}) collective-permute-start(bf16[2048,128]{1,0:T(8,128)(2,1)} %get-tuple-element.20), channel_id=1, source_target_pairs={{3,2},{7,6},{11,10},{15,14},{19,18},{23,22},{27,26},{31,30}} | collective-permute-start | bytes 1572872 | tf_op jit(solution)/shard_map/ppermute | solution.py:206
  81.9 11.9 %collective-permute-start.14 = (bf16[384,128]{1,0:T(8,128)(2,1)S(1)}, bf16[384,128]{1,0:T(8,128)(2,1)S(1)}, u32[]{:S(2)}, u32[]{:S(2)}) collective-permute-start(bf16[384,128]{1,0:T(8,128)(2,1)S(1)} %broadcast_select_fusion.9), channel_id=1, source_target_pairs={{0,2},{1,3},{2,0},{3,1},{4,6},{5,7},{6,4},{7,5},{8,10},{9,11},{10,... | collective-permute-start | bytes 294920 | tf_op jit(solution)/shard_map/ppermute | solution.py:106
  93.9 45.6 %collective-permute-start.15 = (bf16[384,128]{1,0:T(8,128)(2,1)S(1)}, bf16[384,128]{1,0:T(8,128)(2,1)S(1)}, u32[]{:S(2)}, u32[]{:S(2)}) collective-permute-start(bf16[384,128]{1,0:T(8,128)(2,1)S(1)} %add_convert_fusion.10), channel_id=1, source_target_pairs={{0,2},{1,3},{2,0},{3,1},{4,6},{5,7},{6,4},{7,5},{8,10},{9,11},{10,... | collective-permute-start | bytes 294920 | tf_op jit(solution)/shard_map/ppermute | solution.py:106
  110.5 35.1 %collective-permute-start.39 = (bf16[2048,128]{1,0:T(8,128)(2,1)}, bf16[2048,128]{1,0:T(8,128)(2,1)}, u32[]{:S(2)}, u32[]{:S(2)}) collective-permute-start(bf16[2048,128]{1,0:T(8,128)(2,1)} %get-tuple-element.26), channel_id=1, source_target_pairs={{0,1},{4,5},{8,9},{12,13},{16,17},{20,21},{24,25},{28,29}} | collective-permute-start | bytes 1572872 | tf_op jit(solution)/shard_map/ppermute | solution.py:205
  113.1 32.5 %collective-permute-start.42 = (bf16[2048,128]{1,0:T(8,128)(2,1)}, bf16[2048,128]{1,0:T(8,128)(2,1)}, u32[]{:S(2)}, u32[]{:S(2)}) collective-permute-start(bf16[2048,128]{1,0:T(8,128)(2,1)} %get-tuple-element.26), channel_id=1, source_target_pairs={{3,2},{7,6},{11,10},{15,14},{19,18},{23,22},{27,26},{31,30}} | collective-permute-start | bytes 1572872 | tf_op jit(solution)/shard_map/ppermute | solution.py:206
  139.5 12.0 %collective-permute-start.16 = (bf16[768,128]{1,0:T(8,128)(2,1)S(1)}, bf16[768,128]{1,0:T(8,128)(2,1)S(1)}, u32[]{:S(2)}, u32[]{:S(2)}) collective-permute-start(bf16[768,128]{1,0:T(8,128)(2,1)S(1)} %pad_maximum_fusion.8), channel_id=1, source_target_pairs={{0,1},{1,0},{2,3},{3,2},{4,5},{5,4},{6,7},{7,6},{8,9},{9,8},{10,11... | collective-permute-start | bytes 589832 | tf_op jit(solution)/shard_map/ppermute | solution.py:106
  141.1 16.1 %collective-permute-start.26 = (bf16[2048,128]{1,0:T(8,128)(2,1)S(1)}, bf16[2048,128]{1,0:T(8,128)(2,1)S(1)}, u32[]{:S(2)}, u32[]{:S(2)}) collective-permute-start(bf16[2048,128]{1,0:T(8,128)(2,1)S(1)} %get-tuple-element.37), channel_id=1, source_target_pairs={{0,1},{1,2},{4,5},{5,6},{8,9},{9,10},{12,13},{13,14},{16,17},{17,1... | collective-permute-start | bytes 1572872 | tf_op jit(solution)/shard_map/ppermute | solution.py:205
  144.9 12.3 %collective-permute-start.29 = (bf16[2048,128]{1,0:T(8,128)(2,1)S(1)}, bf16[2048,128]{1,0:T(8,128)(2,1)S(1)}, u32[]{:S(2)}, u32[]{:S(2)}) collective-permute-start(bf16[2048,128]{1,0:T(8,128)(2,1)S(1)} %get-tuple-element.38), channel_id=1, source_target_pairs={{2,1},{3,2},{6,5},{7,6},{10,9},{11,10},{14,13},{15,14},{18,17},{19... | collective-permute-start | bytes 1572872 | tf_op jit(solution)/shard_map/ppermute | solution.py:206
  147.3 21.1 %collective-permute-start.40 = (bf16[2048,128]{1,0:T(8,128)(2,1)S(1)}, bf16[2048,128]{1,0:T(8,128)(2,1)S(1)}, u32[]{:S(2)}, u32[]{:S(2)}) collective-permute-start(bf16[2048,128]{1,0:T(8,128)(2,1)S(1)} %get-tuple-element.39), channel_id=1, source_target_pairs={{0,1},{1,2},{4,5},{5,6},{8,9},{9,10},{12,13},{13,14},{16,17},{17,1... | collective-permute-start | bytes 1572872 | tf_op jit(solution)/shard_map/ppermute | solution.py:205
  150.8 17.6 %collective-permute-start.43 = (bf16[2048,128]{1,0:T(8,128)(2,1)S(1)}, bf16[2048,128]{1,0:T(8,128)(2,1)S(1)}, u32[]{:S(2)}, u32[]{:S(2)}) collective-permute-start(bf16[2048,128]{1,0:T(8,128)(2,1)S(1)} %get-tuple-element.40), channel_id=1, source_target_pairs={{2,1},{3,2},{6,5},{7,6},{10,9},{11,10},{14,13},{15,14},{18,17},{19... | collective-permute-start | bytes 1572872 | tf_op jit(solution)/shard_map/ppermute | solution.py:206
  157.7 22.0 %collective-permute-start.27 = (bf16[2048,128]{1,0:T(8,128)(2,1)S(1)}, bf16[2048,128]{1,0:T(8,128)(2,1)S(1)}, u32[]{:S(2)}, u32[]{:S(2)}) collective-permute-start(bf16[2048,128]{1,0:T(8,128)(2,1)S(1)} %get-tuple-element.33), channel_id=1, source_target_pairs={{0,1},{1,2},{2,3},{4,5},{5,6},{6,7},{8,9},{9,10},{10,11},{12,13},{... | collective-permute-start | bytes 1572872 | tf_op jit(solution)/shard_map/ppermute | solution.py:205
  165.0 14.7 %collective-permute-start.30 = (bf16[2048,128]{1,0:T(8,128)(2,1)S(1)}, bf16[2048,128]{1,0:T(8,128)(2,1)S(1)}, u32[]{:S(2)}, u32[]{:S(2)}) collective-permute-start(bf16[2048,128]{1,0:T(8,128)(2,1)S(1)} %get-tuple-element.34), channel_id=1, source_target_pairs={{1,0},{2,1},{3,2},{5,4},{6,5},{7,6},{9,8},{10,9},{11,10},{13,12},{... | collective-permute-start | bytes 1572872 | tf_op jit(solution)/shard_map/ppermute | solution.py:206
  168.9 19.2 %collective-permute-start.41 = (bf16[2048,128]{1,0:T(8,128)(2,1)S(1)}, bf16[2048,128]{1,0:T(8,128)(2,1)}, u32[]{:S(2)}, u32[]{:S(2)}) collective-permute-start(bf16[2048,128]{1,0:T(8,128)(2,1)S(1)} %get-tuple-element.35), channel_id=1, source_target_pairs={{0,1},{1,2},{2,3},{4,5},{5,6},{6,7},{8,9},{9,10},{10,11},{12,13},{... | collective-permute-start | bytes 1572872 | tf_op jit(solution)/shard_map/ppermute | solution.py:205
  176.9 11.2 %collective-permute-start.44 = (bf16[2048,128]{1,0:T(8,128)(2,1)S(1)}, bf16[2048,128]{1,0:T(8,128)(2,1)}, u32[]{:S(2)}, u32[]{:S(2)}) collective-permute-start(bf16[2048,128]{1,0:T(8,128)(2,1)S(1)} %get-tuple-element.36), channel_id=1, source_target_pairs={{1,0},{2,1},{3,2},{5,4},{6,5},{7,6},{9,8},{10,9},{11,10},{13,12},{... | collective-permute-start | bytes 1572872 | tf_op jit(solution)/shard_map/ppermute | solution.py:206
  (36 other events, 275.6 us)

commit v2 on v1

v2 whole, which is shorter than its diff:
```python
import jax
import jax.numpy as jnp
from jax import lax
from jax.experimental import pallas as pl
from jax.experimental.pallas import tpu as pltpu
from jax.sharding import PartitionSpec as P


A = 8
BF = jnp.bfloat16
F32 = jnp.float32


def project_kernel(chunks, block_ref, row_ref, probe_hbm, inverse_hbm, residual_hbm, geno_hbm, *rest):
    outs, (geno, probe, inverse, residual, turned, sems) = rest[:4], rest[4:]
    snps = geno.shape[1]
    tile = snps // chunks
    depth = min(3, chunks)

    def copy(i):
        spot = pl.ds(i * tile, tile)
        return pltpu.make_async_copy(geno_hbm.at[:, spot], geno.at[:, spot], sems.at[i])

    inverse_copy = pltpu.make_async_copy(inverse_hbm.at[0], inverse, sems.at[chunks])
    residual_copy = pltpu.make_async_copy(
        residual_hbm.at[block_ref[0]], residual, sems.at[chunks + 1]
    )
    probe_copy = pltpu.make_async_copy(probe_hbm, probe, sems.at[chunks + 2])
    inverse_copy.start()
    residual_copy.start()
    probe_copy.start()
    for i in range(depth):
        copy(i).start()
    core = row_ref[0] % 2
    chips, part = outs[0].shape[0], outs[0].shape[1]
    span = chips * part

    def spread(h, low, high, lanes):
        mine = jnp.where(core == 0, low, high)
        other = jnp.where(core == 0, high, low).astype(BF)
        for q in range(chips):
            rows = slice(q * part, (q + 1) * part)
            outs[2 * h][q, :, lanes] = mine[rows]
            outs[2 * h + 1][q, :, lanes] = other[rows]

    inverse_copy.wait()
    residual_copy.wait()
    solved = jnp.dot(inverse[...], residual[...].astype(BF), preferred_element_type=F32)
    rhs = solved.shape[1]
    for j in range(solved.shape[0] // (2 * span)):
        lanes = slice(snps + j * rhs, snps + (j + 1) * rhs)
        top = 2 * span * j
        spread(0, solved[top : top + span], solved[top + span : top + 2 * span], lanes)
    probe_copy.wait()
    turned[...] = probe[...].T
    for i in range(chunks):
        copy(i).wait()
        if i + depth < chunks:
            copy(i + depth).start()
        lanes = slice(i * tile, (i + 1) * tile)
        acc = jnp.dot(turned[...], geno[:, lanes], preferred_element_type=F32)
        for h in range(2):
            top = 2 * span * h
            spread(h, acc[top : top + span], acc[top + span : top + 2 * span], lanes)


def project(block, row, probe, inverse, residual, geno, chips):
    rows, snps = geno.shape
    rhs = probe.shape[1]
    part = rhs // (4 * chips)
    chunks = 8
    _, m, g = inverse.shape
    extra = m * rhs // (rhs // 2)
    shapes = []
    for wide in (snps + extra, snps):
        shapes += [
            jax.ShapeDtypeStruct((chips, part, wide), F32),
            jax.ShapeDtypeStruct((chips, part, wide), BF),
        ]

    def kernel(*refs):
        project_kernel(chunks, *refs)

    return pl.pallas_call(
        kernel,
        grid_spec=pltpu.PrefetchScalarGridSpec(
            num_scalar_prefetch=2,
            grid=(1,),
            in_specs=[pl.BlockSpec(memory_space=pltpu.HBM)] * 4,
            out_specs=[pl.BlockSpec(s.shape, lambda i, b, c: (0, 0, 0)) for s in shapes],
            scratch_shapes=[
                pltpu.VMEM((rows, snps), BF),
                pltpu.VMEM((rows, rhs), BF),
                pltpu.VMEM((m, g), BF),
                pltpu.VMEM((g, rhs), F32),
                pltpu.VMEM((rhs, rows), BF),
                pltpu.SemaphoreType.DMA((chunks + 3,)),
            ],
        ),
        out_shape=shapes,
        cost_estimate=pl.CostEstimate(
            flops=2 * rows * snps * rhs, bytes_accessed=2 * rows * snps, transcendentals=0
        ),
        name="project",
    )(block, row, probe, inverse, residual, geno)


def annotate_kernel(ids_of, slices, per_slice, row_ref, col_ref, mine_ref, other_ref, ann_ref, geno_ref, *rest):
    outs, (load, weights) = rest[:slices], rest[slices:]
    chips, part, _ = mine_ref.shape
    width = load.shape[0]

    @pl.when(pl.program_id(0) == 0)
    def _():
        core, chip = row_ref[0] % 2, row_ref[0] // 2
        ids = ids_of(col_ref[0])
        for q in range(chips):
            mine = mine_ref[q ^ chip].astype(F32)
            other = other_ref[q ^ chip].astype(F32)
            load[q * part : (q + 1) * part, :] = jnp.where(core == 0, mine, other)
            low = width // 2 + q * part
            load[low : low + part, :] = jnp.where(core == 0, other, mine)
        for s in range(slices):
            for a in range(per_slice):
                here = ann_ref[...] == ids[s] * per_slice + a
                spot = (s * per_slice + a) * width
                weights[spot : spot + width, :] = jnp.where(here, load[...], 0.0).astype(BF)

    wide = per_slice * width
    acc = lax.dot_general(
        geno_ref[...], weights[...], (((1,), (1,)), ((), ())), preferred_element_type=F32
    )
    for s in range(slices):
        outs[s][...] = acc[:, s * wide : (s + 1) * wide].astype(BF)


def annotate(ids_of, slices, row, col, mine, other, ann, geno, per_slice):
    rows, snps = geno.shape
    chips, part, _ = mine.shape
    width = 2 * chips * part
    wide = per_slice * width
    tile = rows // 2

    def kernel(*refs):
        annotate_kernel(ids_of, slices, per_slice, *refs)

    return pl.pallas_call(
        kernel,
        grid_spec=pltpu.PrefetchScalarGridSpec(
            num_scalar_prefetch=2,
            grid=(rows // tile,),
            in_specs=[
                pl.BlockSpec((chips, part, snps), lambda i, c, d: (0, 0, 0)),
                pl.BlockSpec((chips, part, snps), lambda i, c, d: (0, 0, 0)),
                pl.BlockSpec((1, snps), lambda i, c, d: (0, 0)),
                pl.BlockSpec((tile, snps), lambda i, c, d: (i, 0)),
            ],
            out_specs=[pl.BlockSpec((tile, wide), lambda i, c, d: (i, 0))] * slices,
            scratch_shapes=[pltpu.VMEM((width, snps), F32), pltpu.VMEM((slices * wide, snps), BF)],
        ),
        out_shape=[jax.ShapeDtypeStruct((rows, wide), BF)] * slices,
        cost_estimate=pl.CostEstimate(
            flops=2 * rows * snps * slices * wide, bytes_accessed=2 * rows * snps, transcendentals=0
        ),
        name="annotate",
    )(row, col, mine, other, ann, geno)


def unfold(row, mine, other, snps, rhs):
    chips, part, lanes = mine.shape
    width = 2 * chips * part
    pieces = (lanes - snps) // rhs

    def kernel(row_ref, *refs):
        mine_refs, other_refs, out = refs[:pieces], refs[pieces : 2 * pieces], refs[-1]
        core, chip = row_ref[0] % 2, row_ref[0] // 2
        for j in range(pieces):
            for q in range(chips):
                mine_now = mine_refs[j][q ^ chip].astype(F32)
                other_now = other_refs[j][q ^ chip].astype(F32)
                spot = j * width + q * part
                out[spot : spot + part, :] = jnp.where(core == 0, mine_now, other_now)
                spot += width // 2
                out[spot : spot + part, :] = jnp.where(core == 0, other_now, mine_now)

    first = snps // rhs
    specs = [
        pl.BlockSpec((chips, part, rhs), lambda i, c, j=j: (0, 0, first + j)) for j in range(pieces)
    ]
    return pl.pallas_call(
        kernel,
        grid_spec=pltpu.PrefetchScalarGridSpec(
            num_scalar_prefetch=1,
            grid=(1,),
            in_specs=specs + specs,
            out_specs=pl.BlockSpec((pieces * width, rhs), lambda i, c: (0, 0)),
        ),
        out_shape=jax.ShapeDtypeStruct((pieces * width, rhs), F32),
        name="unfold",
    )(row, *([mine] * pieces), *([other] * pieces))


def flip(x, axis, size, bits):
    return lax.ppermute(x, axis, [(i, i ^ bits) for i in range(size)])


def pick(index, table, choose):
    distinct = sorted(set(table))
    out = choose(distinct[0])
    for p in distinct[1:]:
        here = False
        for i, q in enumerate(table):
            if q == p:
                here = here | (index == i)
        out = jnp.where(here, choose(p), out)
    return out


def make_shards(nr, nc):
    chips = nr // 2

    def row_sum(x, core):
        half = x.shape[0] // 2
        low, high = x[:half], x[half:]
        mine = jnp.where(core == 0, low, high)
        other = jnp.where(core == 0, high, low).astype(BF)
        mine = mine + flip(other, "row", nr, 1).astype(F32)
        sent = mine.astype(BF)
        for q in range(1, chips):
            mine = mine + flip(sent, "row", nr, 2 * q).astype(F32)
        other = flip(mine, "row", nr, 1)
        return jnp.concatenate(
            [jnp.where(core == 0, mine, other), jnp.where(core == 0, other, mine)], axis=0
        )

    def col_sum_small(x):
        sent = x.astype(BF)
        for q in range(1, nc):
            x = x + flip(sent, "col", nc, q).astype(F32)
        return x

    def col_sum_large(x, col):
        parts = x.reshape(nc, x.shape[0] // nc, x.shape[1])
        total = lax.dynamic_index_in_dim(parts, col, 0, keepdims=False).astype(F32)
        for q in range(1, nc):
            piece = lax.dynamic_index_in_dim(parts, col ^ q, 0, keepdims=False)
            total = total + flip(piece, "col", nc, q).astype(F32)
        total = total.astype(BF)
        got = [total] + [flip(total, "col", nc, q) for q in range(1, nc)]
        tables = [[z ^ p for z in range(nc)] for p in range(nc)]
        return jnp.concatenate([pick(col, t, lambda p: got[p]) for t in tables], axis=0)

    def scatter_chips(keep, got, chip, scale, lanes):
        mine = keep + got.astype(F32)
        total = lax.dynamic_index_in_dim(mine, chip, 0, keepdims=False)
        for q in range(1, chips):
            piece = lax.dynamic_index_in_dim(mine, chip ^ q, 0, keepdims=False).astype(BF)
            total = total + flip(piece, "row", nr, 2 * q).astype(F32)
        factor = jnp.where(jnp.arange(total.shape[1]) < lanes, scale, 1.0).astype(F32)
        return (total * factor[None]).astype(BF)

    def gather_plane(total):
        got = [total] + [flip(total, "row", nr, 2 * q) for q in range(1, chips)]
        mine = jnp.stack(got)
        return mine, flip(mine, "row", nr, 1)

    near = nc // 2

    def position(z, s):
        return nc - 1 - s if z < near else s

    def right_table(t):
        return [position(z, nc - 1 - t + z) if z <= t else None for z in range(nc)]

    def left_table(t):
        return [position(z, t - (nc - 1 - z)) if nc - 1 - z <= t else None for z in range(nc)]

    def filled(table):
        some = [p for p in table if p is not None][0]
        return [some if p is None else p for p in table]

    def line_sends(own, t, got, col):
        sends = []
        for side, table in enumerate((right_table(t), left_table(t))):
            send = pick(col, filled(table), lambda p: own[p])
            if t > 0:
                send = (send.astype(F32) + got[side].astype(F32)).astype(BF)
            sends.append(send)
        return sends

    def line_step(sends, t):
        right = [(z, z + 1) for z in range(nc) if z <= t]
        left = [(z, z - 1) for z in range(nc) if nc - 1 - z <= t]
        if t == 0 and nc > 3:
            got = lax.ppermute(sends[0], "col", right + left)
            return got, got
        return lax.ppermute(sends[0], "col", right), lax.ppermute(sends[1], "col", left)

    def line_last(own, got, col):
        last = pick(col, [position(z, z) for z in range(nc)], lambda p: own[p])
        return last.astype(F32) + got[0].astype(F32) + got[1].astype(F32)

    def steps(residual, diag_inverse, panels, first_block, probe_solved, genotypes, annotation):
        nblk, g, rhs = residual.shape
        row = lax.axis_index("row")
        col = lax.axis_index("col")
        core = row % 2
        chip = row // 2
        snps = annotation.shape[0]
        scale = 1.0 / (snps * nc)
        geno = genotypes.reshape(-1, genotypes.shape[2])
        probe = probe_solved.reshape(-1, rhs)
        block_now = first_block[0]
        row_id = row.astype(jnp.int32)[None]
        col_id = col.astype(jnp.int32)[None]
        barrier = lax.optimization_barrier

        keep0, sent0, keep1, sent1 = project(
            first_block, row_id, probe, diag_inverse, residual, geno, chips
        )
        got0 = flip(sent0, "row", nr, 1)
        got1 = flip(sent1, "row", nr, 1)
        total0 = scatter_chips(keep0, got0, chip, scale, snps)
        total0, got1 = barrier((total0, got1))
        load0 = gather_plane(total0)
        total1 = scatter_chips(keep1, got1, chip, scale, snps)

        ann = annotation.reshape(1, -1)
        per_slice = A // nc

        def partials(load, p, count=2):
            def ids_of(z):
                return [jnp.where(z < near, nc - 1 - s, s) for s in range(p, p + count)]

            return annotate(ids_of, count, row_id, col_id, load[0], load[1], ann, geno, per_slice)

        own0 = partials(load0, 0, nc)
        got0 = line_step(line_sends(own0, 0, None, col), 0)
        total1, own0 = barrier((total1, own0))
        load1 = gather_plane(total1)
        solved_load, own0 = barrier((load0, own0))
        first = unfold(row_id, solved_load[0], solved_load[1], snps, rhs)
        first_bf = first.astype(BF)
        own1 = partials(load1, 0)
        got1 = line_step(line_sends(own1, 0, None, col), 0)
        for t in range(1, nc - 1):
            sends = line_sends(own0, t, got0, col)
            got0 = line_step(sends, t)
            if 2 * t < nc:
                load1, sends = barrier((load1, sends))
                own1 = own1 + partials(load1, 2 * t)
            got1 = line_step(line_sends(own1, t, got1, col), t)
        summed = [line_last(own0, got0, col), line_last(own1, got1, col)]

        next_panel = lax.dynamic_index_in_dim(panels[0], block_now + 1, 0, keepdims=False)
        next_sum = col_sum_small(jnp.dot(next_panel, first_bf, preferred_element_type=F32))
        second_rows = lax.dynamic_index_in_dim(residual, block_now + 1, 0, keepdims=False) - next_sum
        second = row_sum(
            jnp.dot(diag_inverse[1], second_rows.astype(BF), preferred_element_type=F32), core
        )
        second_bf = second.astype(BF)
        late = jnp.arange(2, nblk, dtype=jnp.int32)
        keep_first = (late > block_now).astype(F32)[:, None, None]
        keep_second = (late > block_now + 1).astype(F32)[:, None, None]
        both = keep_first * jnp.einsum(
            "ngc,cr->ngr", panels[0, 2:], first_bf, preferred_element_type=F32
        ) + keep_second * jnp.einsum(
            "ngc,cr->ngr", panels[1, 2:], second_bf, preferred_element_type=F32
        )
        update = col_sum_large(both.astype(BF).reshape(-1, rhs), col).reshape(nblk - 2, g, rhs)
        current = jnp.concatenate([residual[:2], residual[2:] - update.astype(F32)], axis=0)
        spot = jnp.arange(nblk, dtype=jnp.int32)[:, None, None] == block_now + 1
        current = jnp.where(spot, second_rows[None], current)

        half = rhs // 2
        products = jnp.stack(summed, axis=1)
        products = products.reshape(nblk, g, 2, per_slice, half)
        products = jnp.swapaxes(products, 2, 3).reshape(nblk, g, per_slice, rhs).astype(BF)
        return current, jnp.stack([first, second]), products

    return steps


def solution(mesh):
    in_specs = (
        P(None, "row", None),
        P(None, "col", "row"),
        P(None, None, "row", "col"),
        P(),
        P(None, "row", None),
        P(None, "row", "col"),
        P("col"),
    )
    out_specs = (P(None, "row", None), P(None, "col", None), P(None, "row", "col", None))
    shards = make_shards(mesh.shape["row"], mesh.shape["col"])
    return jax.shard_map(shards, mesh=mesh, in_specs=in_specs, out_specs=out_specs, check_vma=False)
```

time: 196 us -> 173 us (0.88)
  Pallas kernels: 60.2 us -> 43.1 us
  waiting for transfers between devices: 38.8 us -> 33.9 us
  matrix products: 1.98 us -> 6.48 us
  other arithmetic: 15.7 us -> 11.3 us
    pallas_call x4 -> x3, Pallas kernels: 49.5 us -> 33.1 us  [annotate(): pl.pallas_call(kernel, grid_spec=pltpu.PrefetchScalarGridSpec(num_scalar_...]
    ppermute x12 -> x10, waiting for transfers between devices: 15.6 us -> 8.47 us  [the longest x4 4.91 us: line_step(): lax.ppermute(sends[1], 'col', left)]
    dot_general x5 -> x4, matrix products: 1.98 us -> 6.48 us  [the longest x1 2.07 us: steps(): jnp.einsum('ngc,cr->ngr', panels[0, 2:], first_bf, preferred_element_type...]
    concatenate x6 -> x1, other arithmetic: 3.14 us -> 0.03 us  [col_sum_large(): jnp.concatenate([pick(col, t, lambda p: got[p]) for t in tables], axis=0)]
    convert_element_type x11 -> x10, other arithmetic: 4.25 us -> 7.11 us  [the longest x4 6.86 us: line_sends(): send = (send.astype(F32) + got[side].astype(F32)).astype(BF)]
    ppermute x33 -> x30, waiting for transfers between devices: 23.1 us -> 25.4 us  [flip(): return lax.ppermute(x, axis, [(i, i ^ bits) for i in range(size)])]
    select_n x7 -> x3, other arithmetic: 3.37 us -> 1.13 us  [the longest x1 1.12 us: steps(): current = jnp.where(spot, second_rows[None], current)]
    pallas_call x1 -> x2, Pallas kernels: 10.6 us -> 9.96 us  [the longest x1 8.24 us: project(): pl.pallas_call(kernel, grid_spec=pltpu.PrefetchScalarGridSpec(num_scalar_...]
  transfers between devices with their start and end apart: 45 -> 40, of which waited for: 18 -> 19; matrix products, arithmetic and copies ran while one was open for 10% -> 9% of each run, Pallas kernels for 26% -> 11%
where the time goes in v2:
time: 173 us; the launch traced here: 171 us
  starting transfers between devices  69.3 us (40%)
  Pallas kernels  43.1 us (25%)
  waiting for transfers between devices  33.9 us (20%)
  other arithmetic  11.3 us (7%)
  matrix products  6.48 us (4%)
  local copies, waits for them, and re-layouts  4.79 us (3%)
  between operations  1.86 us (1%)
    ppermute x30, starting transfers between devices, flip(): return lax.ppermute(x, axis, [(i, i ^ bits) for i in range(size)])  33.2 us
    pallas_call x3, Pallas kernels, annotate(): pl.pallas_call(kernel, grid_spec=pltpu.PrefetchScalarGridSpec(num_scalar_...  33.1 us
    ppermute x4, starting transfers between devices, line_step(): lax.ppermute(sends[0], 'col', right)  27.2 us
    ppermute x30, waiting for transfers between devices, flip(): return lax.ppermute(x, axis, [(i, i ^ bits) for i in range(size)])  25.4 us
    pallas_call x1, Pallas kernels, project(): pl.pallas_call(kernel, grid_spec=pltpu.PrefetchScalarGridSpec(num_scalar_...  8.24 us
    convert_element_type x4, other arithmetic, line_sends(): send = (send.astype(F32) + got[side].astype(F32)).astype(BF)  6.86 us
    ppermute x4, waiting for transfers between devices, line_step(): lax.ppermute(sends[1], 'col', left)  4.91 us
    ppermute x2, starting transfers between devices, line_step(): got = lax.ppermute(sends[0], 'col', right + left)  4.8 us
  transfers between devices with their start and end apart: 40, of which 19 were waited for; matrix products, arithmetic and copies ran while one was open for 9% of the time, Pallas kernels for 11%

profile of v2, /device:TPU:0, one launch (start us, length us, event | category | flops | bytes accessed | tf_op | source)
XLA Modules:
  0.0 170.8 jit_solution(6585304286636152768)
XLA Ops:
  1.3 8.2 %project.1 = (f32[4,8,5120]{2,1,0:T(8,128)}, bf16[4,8,5120]{2,1,0:T(8,128)(2,1)}, f32[4,8,4096]{2,1,0:T(8,128)}, bf16[4,8,4096]{2,1,0:T(8,128)(2,1)}) custom-call(s32[1]{0:T(128)} %copy.29.refs_0_, s32[1]{0:T(128)} %bitcast.3.refs_1_.refs_0_.row_ref, bf16[2048,128]{1,0:T(8,128)(2,1)} %bitcast.126, bf16[2,512,256]{2,1,0:T(8,128)(2,1)} %refs_3_.1, ...), custom_call_target="tpu_custom_call" | custom-call | flops 2147483648 | bytes 16777216 | tf_op jit(solution)/shard_map/project/pallas_call | solution.py:84
  11.7 2.9 %collective-permute-start.1 = (bf16[8,5120]{1,0:T(8,128)(2,1)S(1)}, bf16[8,5120]{1,0:T(8,128)(2,1)S(1)}, u32[]{:S(2)}, u32[]{:S(2)}) collective-permute-start(bf16[8,5120]{1,0:T(8,128)(2,1)S(1)} %get-tuple-element.68), channel_id=1, source_target_pairs={{0,8},{4,12},{8,0},{12,4},{16,24},{20,28},{24,16},{28,20},{1,9},{5... | collective-permute-start | bytes 245768 | tf_op jit(solution)/shard_map/ppermute | solution.py:204
  17.3 2.5 %collective-permute-done.2 = bf16[8,5120]{1,0:T(8,128)(2,1)S(1)} collective-permute-done((bf16[8,5120]{1,0:T(8,128)(2,1)S(1)}, bf16[8,5120]{1,0:T(8,128)(2,1)S(1)}, u32[]{:S(2)}, u32[]{:S(2)}) %collective-permute-start.2) | collective-permute-done | bytes 81952 | tf_op jit(solution)/shard_map/ppermute | solution.py:204
  22.9 2.2 %collective-permute-start.7 = (bf16[8,5120]{1,0:T(8,128)(2,1)S(1)}, bf16[8,5120]{1,0:T(8,128)(2,1)S(1)}, u32[]{:S(2)}, u32[]{:S(2)}) collective-permute-start(bf16[8,5120]{1,0:T(8,128)(2,1)S(1)} %fusion.38), channel_id=1, source_target_pairs={{0,24},{4,28},{8,16},{12,20},{16,8},{20,12},{24,0},{28,4},{1,25},{... | collective-permute-start | bytes 245768 | tf_op jit(solution)/shard_map/ppermute | solution.py:204
  32.4 14.3 %annotate.3 = (bf16[2048,128]{1,0:T(8,128)(2,1)}, bf16[2048,128]{1,0:T(8,128)(2,1)}, bf16[2048,128]{1,0:T(8,128)(2,1)}, bf16[2048,128]{1,0:T(8,128)(2,1)}) custom-call(s32[1]{0:T(128)} %bitcast.3.refs_1_.refs_0_.row_ref, s32[1]{0:T(128)} %bitcast.18.refs_1_, bf16[4,8,5120]{2,1,0:T(8,128)(2,1)} %copy-done, bf16[4,8,5120]{2,1,0:T(8,128)(2,1)} %copy-done.1, ...), custom_call_target="tpu_custom_call" | custom-call | flops 8589934592 | bytes 16777216 | tf_op jit(solution)/shard_map/annotate/pallas_call | solution.py:147
  51.2 2.6 %collective-permute-start.13 = (bf16[256,128]{1,0:T(8,128)(2,1)S(1)}, bf16[256,128]{1,0:T(8,128)(2,1)S(1)}, u32[]{:S(2)}, u32[]{:S(2)}) collective-permute-start(bf16[256,128]{1,0:T(8,128)(2,1)S(1)} %get-tuple-element.83), channel_id=1, source_target_pairs={{0,2},{1,3},{2,0},{3,1},{4,6},{5,7},{6,4},{7,5},{8,10},{9,11},{10,... | collective-permute-start | bytes 196616 | tf_op jit(solution)/shard_map/ppermute | solution.py:204
  57.8 2.1 %collective-permute-done.14 = bf16[256,128]{1,0:T(8,128)(2,1)S(1)} collective-permute-done((bf16[256,128]{1,0:T(8,128)(2,1)S(1)}, bf16[256,128]{1,0:T(8,128)(2,1)S(1)}, u32[]{:S(2)}, u32[]{:S(2)}) %collective-permute-start.14) | collective-permute-done | bytes 65568 | tf_op jit(solution)/shard_map/ppermute | solution.py:204
  66.0 2.5 %collective-permute-start.26 = (bf16[2048,128]{1,0:T(8,128)(2,1)}, bf16[2048,128]{1,0:T(8,128)(2,1)}, u32[]{:S(2)}, u32[]{:S(2)}) collective-permute-start(bf16[2048,128]{1,0:T(8,128)(2,1)} %get-tuple-element.49), channel_id=1, source_target_pairs={{0,1},{3,2},{4,5},{7,6},{8,9},{11,10},{12,13},{15,14},{16,17},{19,... | collective-permute-start | bytes 1572872 | tf_op jit(solution)/shard_map/ppermute | solution.py:295
  70.8 9.4 %annotate.5 = (bf16[2048,128]{1,0:T(8,128)(2,1)}, bf16[2048,128]{1,0:T(8,128)(2,1)}) custom-call(s32[1]{0:T(128)} %bitcast.3.refs_1_.refs_0_.row_ref, s32[1]{0:T(128)} %bitcast.18.refs_1_, bf16[4,8,4096]{2,1,0:T(8,128)(2,1)} %copy-done.4, bf16[4,8,4096]{2,1,0:T(8,128)(2,1)} %copy-done.11, s32[1,4096]{1,0:T(1,128)} %bitcast.133, bf16[2048,4096]{1,0:T(8,128)(2,1)} %bitcast.115), custom_call_target="tpu_custom_call" | custom-call | flops 4294967296 | bytes 16777216 | tf_op jit(solution)/shard_map/annotate/pallas_call | solution.py:147
  80.2 2.3 %collective-permute-start.35 = (bf16[2048,128]{1,0:T(8,128)(2,1)}, bf16[2048,128]{1,0:T(8,128)(2,1)}, u32[]{:S(2)}, u32[]{:S(2)}) collective-permute-start(bf16[2048,128]{1,0:T(8,128)(2,1)} %get-tuple-element.56), channel_id=1, source_target_pairs={{0,1},{3,2},{4,5},{7,6},{8,9},{11,10},{12,13},{15,14},{16,17},{19,... | collective-permute-start | bytes 1572872 | tf_op jit(solution)/shard_map/ppermute | solution.py:295
  84.6 2.1 %fusion.18 = bf16[6,256,128]{1,2,0:T(8,128)(2,1)S(1)} fusion(f32[128,6,256]{2,0,1:T(8,128)S(1)} %fusion.12, bf16[2,8,256,512]{3,2,1,0:T(8,128)(2,1)} %param.9, f32[6]{0:T(128)S(1)} %compare_convert_fusion.1, f32[512,128]{1,0:T(8,128)S(1)} %copy-done.3), kind=kOutput, calls=%fused_computation.14 | convolution fusion | flops 201981952 | bytes 3014680 | tf_op jit(solution)/shard_map/ngc,cr->ngr/dot_general | solution.py:365
  87.1 3.7 %collective-permute-start.21 = (bf16[384,128]{1,0:T(8,128)(2,1)S(1)}, bf16[384,128]{1,0:T(8,128)(2,1)S(1)}, u32[]{:S(2)}, u32[]{:S(2)}) collective-permute-start(bf16[384,128]{1,0:T(8,128)(2,1)S(1)} %get-tuple-element.80), channel_id=1, source_target_pairs={{0,2},{1,3},{2,0},{3,1},{4,6},{5,7},{6,4},{7,5},{8,10},{9,11},{10,... | collective-permute-start | bytes 294920 | tf_op jit(solution)/shard_map/ppermute | solution.py:204
  92.3 4.0 %collective-permute-done.20 = bf16[384,128]{1,0:T(8,128)(2,1)S(1)} collective-permute-done((bf16[384,128]{1,0:T(8,128)(2,1)S(1)}, bf16[384,128]{1,0:T(8,128)(2,1)S(1)}, u32[]{:S(2)}, u32[]{:S(2)}) %collective-permute-start.20) | collective-permute-done | bytes 98336 | tf_op jit(solution)/shard_map/ppermute | solution.py:204
  96.3 2.1 %collective-permute-done.21 = bf16[384,128]{1,0:T(8,128)(2,1)S(1)} collective-permute-done((bf16[384,128]{1,0:T(8,128)(2,1)S(1)}, bf16[384,128]{1,0:T(8,128)(2,1)S(1)}, u32[]{:S(2)}, u32[]{:S(2)}) %collective-permute-start.21) | collective-permute-done | bytes 98336 | tf_op jit(solution)/shard_map/ppermute | solution.py:204
  98.4 5.3 %collective-permute-done.22 = bf16[384,128]{1,0:T(8,128)(2,1)S(1)} collective-permute-done((bf16[384,128]{1,0:T(8,128)(2,1)S(1)}, bf16[384,128]{1,0:T(8,128)(2,1)S(1)}, u32[]{:S(2)}, u32[]{:S(2)}) %collective-permute-start.22) | collective-permute-done | bytes 98336 | tf_op jit(solution)/shard_map/ppermute | solution.py:204
  104.6 3.6 %collective-permute-start.25 = (bf16[384,128]{1,0:T(8,128)(2,1)S(1)}, bf16[384,128]{1,0:T(8,128)(2,1)S(1)}, u32[]{:S(2)}, u32[]{:S(2)}) collective-permute-start(bf16[384,128]{1,0:T(8,128)(2,1)S(1)} %fusion.34), channel_id=1, source_target_pairs={{0,1},{1,0},{2,3},{3,2},{4,5},{5,4},{6,7},{7,6},{8,9},{9,8},{10,11... | collective-permute-start | bytes 294920 | tf_op jit(solution)/shard_map/ppermute | solution.py:204
  108.2 2.5 %fusion.22 = (bf16[2048,128]{1,0:T(8,128)(2,1)}, bf16[2048,128]{1,0:T(8,128)(2,1)}) fusion(bf16[2048,128]{1,0:T(8,128)(2,1)} %collective-permute-done.26, bf16[2048,128]{1,0:T(8,128)(2,1)S(1)} %copy-done.5, bf16[2048,128]{1,0:T(8,128)(2,1)} %get-tuple-element.49, pred[]{:T(512)S(6)} %eq.23, pred[]{:T(512)S(6)} %or.20), kind=kLoop, calls=%fused_computation.17 | loop fusion | flops 2359296 | bytes 2621442 | tf_op jit(solution)/shard_map/convert_element_type | solution.py:287
  110.7 2.7 %collective-permute-start.27 = (bf16[2048,128]{1,0:T(8,128)(2,1)}, bf16[2048,128]{1,0:T(8,128)(2,1)}, u32[]{:S(2)}, u32[]{:S(2)}) collective-permute-start(bf16[2048,128]{1,0:T(8,128)(2,1)} %get-tuple-element.67), channel_id=1, source_target_pairs={{0,1},{1,2},{4,5},{5,6},{8,9},{9,10},{12,13},{13,14},{16,17},{17,1... | collective-permute-start | bytes 1572872 | tf_op jit(solution)/shard_map/ppermute | solution.py:297
  113.4 9.5 %annotate.4 = (bf16[2048,128]{1,0:T(8,128)(2,1)}, bf16[2048,128]{1,0:T(8,128)(2,1)}) custom-call(s32[1]{0:T(128)} %bitcast.3.refs_1_.refs_0_.row_ref, s32[1]{0:T(128)} %bitcast.18.refs_1_, bf16[4,8,4096]{2,1,0:T(8,128)(2,1)} %copy-done.4, bf16[4,8,4096]{2,1,0:T(8,128)(2,1)} %copy-done.11, s32[1,4096]{1,0:T(1,128)} %bitcast.134, bf16[2048,4096]{1,0:T(8,128)(2,1)} %bitcast.116), custom_call_target="tpu_custom_call" | custom-call | flops 4294967296 | bytes 16777216 | tf_op jit(solution)/shard_map/annotate/pallas_call | solution.py:147
  125.5 2.3 %collective-permute-start.36 = (bf16[2048,128]{1,0:T(8,128)(2,1)S(1)}, bf16[2048,128]{1,0:T(8,128)(2,1)S(1)}, u32[]{:S(2)}, u32[]{:S(2)}) collective-permute-start(bf16[2048,128]{1,0:T(8,128)(2,1)S(1)} %get-tuple-element.64), channel_id=1, source_target_pairs={{0,1},{1,2},{4,5},{5,6},{8,9},{9,10},{12,13},{13,14},{16,17},{17,1... | collective-permute-start | bytes 1572872 | tf_op jit(solution)/shard_map/ppermute | solution.py:297
  130.1 13.2 %collective-permute-start.28 = (bf16[2048,128]{1,0:T(8,128)(2,1)S(1)}, bf16[2048,128]{1,0:T(8,128)(2,1)S(1)}, u32[]{:S(2)}, u32[]{:S(2)}) collective-permute-start(bf16[2048,128]{1,0:T(8,128)(2,1)S(1)} %get-tuple-element.60), channel_id=1, source_target_pairs={{0,1},{1,2},{2,3},{4,5},{5,6},{6,7},{8,9},{9,10},{10,11},{12,13},{... | collective-permute-start | bytes 1572872 | tf_op jit(solution)/shard_map/ppermute | solution.py:297
  146.1 9.0 %collective-permute-start.37 = (bf16[2048,128]{1,0:T(8,128)(2,1)}, bf16[2048,128]{1,0:T(8,128)(2,1)}, u32[]{:S(2)}, u32[]{:S(2)}) collective-permute-start(bf16[2048,128]{1,0:T(8,128)(2,1)} %get-tuple-element.62), channel_id=1, source_target_pairs={{0,1},{1,2},{2,3},{4,5},{5,6},{6,7},{8,9},{9,10},{10,11},{12,13},{... | collective-permute-start | bytes 1572872 | tf_op jit(solution)/shard_map/ppermute | solution.py:297
  158.1 3.5 %collective-permute-done.37 = bf16[2048,128]{1,0:T(8,128)(2,1)} collective-permute-done((bf16[2048,128]{1,0:T(8,128)(2,1)}, bf16[2048,128]{1,0:T(8,128)(2,1)}, u32[]{:S(2)}, u32[]{:S(2)}) %collective-permute-start.37) | collective-permute-done | bytes 524320 | tf_op jit(solution)/shard_map/ppermute | solution.py:297
  161.7 4.9 %collective-permute-done.39 = bf16[2048,128]{1,0:T(8,128)(2,1)} collective-permute-done((bf16[2048,128]{1,0:T(8,128)(2,1)}, bf16[2048,128]{1,0:T(8,128)(2,1)}, u32[]{:S(2)}, u32[]{:S(2)}) %collective-permute-start.39) | collective-permute-done | bytes 524320 | tf_op jit(solution)/shard_map/ppermute | solution.py:297
  (139 shorter events, 51.5 us)
Async XLA Ops:
  10.1 11.4 %collective-permute-start.4 = (bf16[4,8,4096]{2,1,0:T(8,128)(2,1)}, bf16[4,8,4096]{2,1,0:T(8,128)(2,1)S(1)}, u32[]{:S(2)}, u32[]{:S(2)}) collective-permute-start(bf16[4,8,4096]{2,1,0:T(8,128)(2,1)} %get-tuple-element.32), channel_id=1, source_target_pairs={{0,4},{4,0},{8,12},{12,8},{16,20},{20,16},{24,28},{28,24},{1,5},{5... | collective-permute-start | bytes 786440 | tf_op jit(solution)/shard_map/ppermute | solution.py:204
  22.1 6.8 %collective-permute-start.6 = (bf16[8,5120]{1,0:T(8,128)(2,1)S(1)}, bf16[8,5120]{1,0:T(8,128)(2,1)S(1)}, u32[]{:S(2)}, u32[]{:S(2)}) collective-permute-start(bf16[8,5120]{1,0:T(8,128)(2,1)S(1)} %fusion.38), channel_id=1, source_target_pairs={{0,16},{4,20},{8,24},{12,28},{16,0},{20,4},{24,8},{28,12},{1,17},{... | collective-permute-start | bytes 245768 | tf_op jit(solution)/shard_map/ppermute | solution.py:204
  49.6 6.7 %collective-permute-start.12 = (bf16[256,128]{1,0:T(8,128)(2,1)S(1)}, bf16[256,128]{1,0:T(8,128)(2,1)S(1)}, u32[]{:S(2)}, u32[]{:S(2)}) collective-permute-start(bf16[256,128]{1,0:T(8,128)(2,1)S(1)} %get-tuple-element.83), channel_id=1, source_target_pairs={{0,1},{1,0},{2,3},{3,2},{4,5},{5,4},{6,7},{7,6},{8,9},{9,8},{10,11... | collective-permute-start | bytes 196616 | tf_op jit(solution)/shard_map/ppermute | solution.py:204
  51.2 6.6 %collective-permute-start.13 = (bf16[256,128]{1,0:T(8,128)(2,1)S(1)}, bf16[256,128]{1,0:T(8,128)(2,1)S(1)}, u32[]{:S(2)}, u32[]{:S(2)}) collective-permute-start(bf16[256,128]{1,0:T(8,128)(2,1)S(1)} %get-tuple-element.83), channel_id=1, source_target_pairs={{0,2},{1,3},{2,0},{3,1},{4,6},{5,7},{6,4},{7,5},{8,10},{9,11},{10,... | collective-permute-start | bytes 196616 | tf_op jit(solution)/shard_map/ppermute | solution.py:204
  53.8 6.1 %collective-permute-start.14 = (bf16[256,128]{1,0:T(8,128)(2,1)S(1)}, bf16[256,128]{1,0:T(8,128)(2,1)S(1)}, u32[]{:S(2)}, u32[]{:S(2)}) collective-permute-start(bf16[256,128]{1,0:T(8,128)(2,1)S(1)} %get-tuple-element.83), channel_id=1, source_target_pairs={{0,3},{1,2},{2,1},{3,0},{4,7},{5,6},{6,5},{7,4},{8,11},{9,10},{10,... | collective-permute-start | bytes 196616 | tf_op jit(solution)/shard_map/ppermute | solution.py:204
  54.0 7.2 %collective-permute-start.31 = (bf16[8,4096]{1,0:T(8,128)(2,1)S(1)}, bf16[8,4096]{1,0:T(8,128)(2,1)S(1)}, u32[]{:S(2)}, u32[]{:S(2)}) collective-permute-start(bf16[8,4096]{1,0:T(8,128)(2,1)S(1)} %fusion.45), channel_id=1, source_target_pairs={{0,8},{4,12},{8,0},{12,4},{16,24},{20,28},{24,16},{28,20},{1,9},{5... | collective-permute-start | bytes 196616 | tf_op jit(solution)/shard_map/ppermute | solution.py:204
  61.5 8.6 %collective-permute-start.34 = (bf16[4,8,4096]{2,1,0:T(8,128)(2,1)S(1)}, bf16[4,8,4096]{2,1,0:T(8,128)(2,1)S(1)}, u32[]{:S(2)}, u32[]{:S(2)}) collective-permute-start(bf16[4,8,4096]{2,1,0:T(8,128)(2,1)S(1)} %pad_maximum_fusion.4.refs_2_), channel_id=1, source_target_pairs={{0,4},{4,0},{8,12},{12,8},{16,20},{20,16},{24,28},{28,24},{1,5},{5... | collective-permute-start | bytes 786440 | tf_op jit(solution)/shard_map/ppermute | solution.py:204
  62.5 6.0 %collective-permute-start.16 = (bf16[256,128]{1,0:T(8,128)(2,1)S(1)}, bf16[256,128]{1,0:T(8,128)(2,1)S(1)}, u32[]{:S(2)}, u32[]{:S(2)}) collective-permute-start(bf16[256,128]{1,0:T(8,128)(2,1)S(1)} %fusion.58), channel_id=1, source_target_pairs={{0,8},{4,12},{8,0},{12,4},{16,24},{20,28},{24,16},{28,20},{1,9},{5... | collective-permute-start | bytes 196616 | tf_op jit(solution)/shard_map/ppermute | solution.py:204
  66.0 42.2 %collective-permute-start.26 = (bf16[2048,128]{1,0:T(8,128)(2,1)}, bf16[2048,128]{1,0:T(8,128)(2,1)}, u32[]{:S(2)}, u32[]{:S(2)}) collective-permute-start(bf16[2048,128]{1,0:T(8,128)(2,1)} %get-tuple-element.49), channel_id=1, source_target_pairs={{0,1},{3,2},{4,5},{7,6},{8,9},{11,10},{12,13},{15,14},{16,17},{19,... | collective-permute-start | bytes 1572872 | tf_op jit(solution)/shard_map/ppermute | solution.py:295
  70.0 12.6 %collective-permute-start.19 = (f32[256,128]{1,0:T(8,128)S(1)}, f32[256,128]{1,0:T(8,128)S(1)}, u32[]{:S(2)}, u32[]{:S(2)}) collective-permute-start(f32[256,128]{1,0:T(8,128)S(1)} %convert_add_fusion.7), channel_id=1, source_target_pairs={{0,4},{4,0},{8,12},{12,8},{16,20},{20,16},{24,28},{28,24},{1,5},{5... | collective-permute-start | bytes 393224 | tf_op jit(solution)/shard_map/ppermute | solution.py:204
  80.2 43.8 %collective-permute-start.35 = (bf16[2048,128]{1,0:T(8,128)(2,1)}, bf16[2048,128]{1,0:T(8,128)(2,1)}, u32[]{:S(2)}, u32[]{:S(2)}) collective-permute-start(bf16[2048,128]{1,0:T(8,128)(2,1)} %get-tuple-element.56), channel_id=1, source_target_pairs={{0,1},{3,2},{4,5},{7,6},{8,9},{11,10},{12,13},{15,14},{16,17},{19,... | collective-permute-start | bytes 1572872 | tf_op jit(solution)/shard_map/ppermute | solution.py:295
  87.0 9.3 %collective-permute-start.20 = (bf16[384,128]{1,0:T(8,128)(2,1)S(1)}, bf16[384,128]{1,0:T(8,128)(2,1)S(1)}, u32[]{:S(2)}, u32[]{:S(2)}) collective-permute-start(bf16[384,128]{1,0:T(8,128)(2,1)S(1)} %get-tuple-element.78), channel_id=1, source_target_pairs={{0,1},{1,0},{2,3},{3,2},{4,5},{5,4},{6,7},{7,6},{8,9},{9,8},{10,11... | collective-permute-start | bytes 294920 | tf_op jit(solution)/shard_map/ppermute | solution.py:204
  87.1 11.4 %collective-permute-start.21 = (bf16[384,128]{1,0:T(8,128)(2,1)S(1)}, bf16[384,128]{1,0:T(8,128)(2,1)S(1)}, u32[]{:S(2)}, u32[]{:S(2)}) collective-permute-start(bf16[384,128]{1,0:T(8,128)(2,1)S(1)} %get-tuple-element.80), channel_id=1, source_target_pairs={{0,2},{1,3},{2,0},{3,1},{4,6},{5,7},{6,4},{7,5},{8,10},{9,11},{10,... | collective-permute-start | bytes 294920 | tf_op jit(solution)/shard_map/ppermute | solution.py:204
  90.8 12.9 %collective-permute-start.22 = (bf16[384,128]{1,0:T(8,128)(2,1)S(1)}, bf16[384,128]{1,0:T(8,128)(2,1)S(1)}, u32[]{:S(2)}, u32[]{:S(2)}) collective-permute-start(bf16[384,128]{1,0:T(8,128)(2,1)S(1)} %get-tuple-element.79), channel_id=1, source_target_pairs={{0,3},{1,2},{2,1},{3,0},{4,7},{5,6},{6,5},{7,4},{8,11},{9,10},{10,... | collective-permute-start | bytes 294920 | tf_op jit(solution)/shard_map/ppermute | solution.py:204
  103.8 19.1 %collective-permute-start.23 = (bf16[384,128]{1,0:T(8,128)(2,1)S(1)}, bf16[384,128]{1,0:T(8,128)(2,1)S(1)}, u32[]{:S(2)}, u32[]{:S(2)}) collective-permute-start(bf16[384,128]{1,0:T(8,128)(2,1)S(1)} %fusion.34), channel_id=1, source_target_pairs={{0,3},{1,2},{2,1},{3,0},{4,7},{5,6},{6,5},{7,4},{8,11},{9,10},{10,... | collective-permute-start | bytes 294920 | tf_op jit(solution)/shard_map/ppermute | solution.py:204
  104.6 19.1 %collective-permute-start.24 = (bf16[384,128]{1,0:T(8,128)(2,1)S(1)}, bf16[384,128]{1,0:T(8,128)(2,1)S(1)}, u32[]{:S(2)}, u32[]{:S(2)}) collective-permute-start(bf16[384,128]{1,0:T(8,128)(2,1)S(1)} %fusion.34), channel_id=1, source_target_pairs={{0,2},{1,3},{2,0},{3,1},{4,6},{5,7},{6,4},{7,5},{8,10},{9,11},{10,... | collective-permute-start | bytes 294920 | tf_op jit(solution)/shard_map/ppermute | solution.py:204
  104.6 19.1 %collective-permute-start.25 = (bf16[384,128]{1,0:T(8,128)(2,1)S(1)}, bf16[384,128]{1,0:T(8,128)(2,1)S(1)}, u32[]{:S(2)}, u32[]{:S(2)}) collective-permute-start(bf16[384,128]{1,0:T(8,128)(2,1)S(1)} %fusion.34), channel_id=1, source_target_pairs={{0,1},{1,0},{2,3},{3,2},{4,5},{5,4},{6,7},{7,6},{8,9},{9,8},{10,11... | collective-permute-start | bytes 294920 | tf_op jit(solution)/shard_map/ppermute | solution.py:204
  110.7 17.9 %collective-permute-start.27 = (bf16[2048,128]{1,0:T(8,128)(2,1)}, bf16[2048,128]{1,0:T(8,128)(2,1)}, u32[]{:S(2)}, u32[]{:S(2)}) collective-permute-start(bf16[2048,128]{1,0:T(8,128)(2,1)} %get-tuple-element.67), channel_id=1, source_target_pairs={{0,1},{1,2},{4,5},{5,6},{8,9},{9,10},{12,13},{13,14},{16,17},{17,1... | collective-permute-start | bytes 1572872 | tf_op jit(solution)/shard_map/ppermute | solution.py:297
  125.5 19.1 %collective-permute-start.36 = (bf16[2048,128]{1,0:T(8,128)(2,1)S(1)}, bf16[2048,128]{1,0:T(8,128)(2,1)S(1)}, u32[]{:S(2)}, u32[]{:S(2)}) collective-permute-start(bf16[2048,128]{1,0:T(8,128)(2,1)S(1)} %get-tuple-element.64), channel_id=1, source_target_pairs={{0,1},{1,2},{4,5},{5,6},{8,9},{9,10},{12,13},{13,14},{16,17},{17,1... | collective-permute-start | bytes 1572872 | tf_op jit(solution)/shard_map/ppermute | solution.py:297
  127.9 16.7 %collective-permute-start.38 = (bf16[2048,128]{1,0:T(8,128)(2,1)S(1)}, bf16[2048,128]{1,0:T(8,128)(2,1)S(1)}, u32[]{:S(2)}, u32[]{:S(2)}) collective-permute-start(bf16[2048,128]{1,0:T(8,128)(2,1)S(1)} %get-tuple-element.65), channel_id=1, source_target_pairs={{2,1},{3,2},{6,5},{7,6},{10,9},{11,10},{14,13},{15,14},{18,17},{19... | collective-permute-start | bytes 1572872 | tf_op jit(solution)/shard_map/ppermute | solution.py:297
  130.1 27.4 %collective-permute-start.28 = (bf16[2048,128]{1,0:T(8,128)(2,1)S(1)}, bf16[2048,128]{1,0:T(8,128)(2,1)S(1)}, u32[]{:S(2)}, u32[]{:S(2)}) collective-permute-start(bf16[2048,128]{1,0:T(8,128)(2,1)S(1)} %get-tuple-element.60), channel_id=1, source_target_pairs={{0,1},{1,2},{2,3},{4,5},{5,6},{6,7},{8,9},{9,10},{10,11},{12,13},{... | collective-permute-start | bytes 1572872 | tf_op jit(solution)/shard_map/ppermute | solution.py:297
  143.3 14.2 %collective-permute-start.30 = (bf16[2048,128]{1,0:T(8,128)(2,1)S(1)}, bf16[2048,128]{1,0:T(8,128)(2,1)S(1)}, u32[]{:S(2)}, u32[]{:S(2)}) collective-permute-start(bf16[2048,128]{1,0:T(8,128)(2,1)S(1)} %get-tuple-element.61), channel_id=1, source_target_pairs={{1,0},{2,1},{3,2},{5,4},{6,5},{7,6},{9,8},{10,9},{11,10},{13,12},{... | collective-permute-start | bytes 1572872 | tf_op jit(solution)/shard_map/ppermute | solution.py:297
  146.1 15.6 %collective-permute-start.37 = (bf16[2048,128]{1,0:T(8,128)(2,1)}, bf16[2048,128]{1,0:T(8,128)(2,1)}, u32[]{:S(2)}, u32[]{:S(2)}) collective-permute-start(bf16[2048,128]{1,0:T(8,128)(2,1)} %get-tuple-element.62), channel_id=1, source_target_pairs={{0,1},{1,2},{2,3},{4,5},{5,6},{6,7},{8,9},{9,10},{10,11},{12,13},{... | collective-permute-start | bytes 1572872 | tf_op jit(solution)/shard_map/ppermute | solution.py:297
  155.1 11.5 %collective-permute-start.39 = (bf16[2048,128]{1,0:T(8,128)(2,1)}, bf16[2048,128]{1,0:T(8,128)(2,1)}, u32[]{:S(2)}, u32[]{:S(2)}) collective-permute-start(bf16[2048,128]{1,0:T(8,128)(2,1)} %get-tuple-element.63), channel_id=1, source_target_pairs={{1,0},{2,1},{3,2},{5,4},{6,5},{7,6},{9,8},{10,9},{11,10},{13,12},{... | collective-permute-start | bytes 1572872 | tf_op jit(solution)/shard_map/ppermute | solution.py:297
  (33 other events, 221.2 us)

commit v3 on v2

--- a/solution.py
+++ b/solution.py
@@ -266,27 +266,36 @@
 
     near = nc // 2
 
-    def position(z, s):
-        return nc - 1 - s if z < near else s
+    def slice_order(z):
+        if nc == 4:
+            return [[3, 2, 1, 0], [0, 3, 2, 1], [3, 0, 1, 2], [0, 1, 2, 3]][z]
+        return [nc - 1 - p if z < near else p for p in range(nc)]
+
+    orders = [slice_order(z) for z in range(nc)]
 
     def right_table(t):
-        return [position(z, nc - 1 - t + z) if z <= t else None for z in range(nc)]
+        return [orders[z].index(nc - 1 - t + z) if z <= t else None for z in range(nc)]
 
     def left_table(t):
-        return [position(z, t - (nc - 1 - z)) if nc - 1 - z <= t else None for z in range(nc)]
+        return [orders[z].index(t - (nc - 1 - z)) if nc - 1 - z <= t else None for z in range(nc)]
 
     def filled(table):
         some = [p for p in table if p is not None][0]
         return [some if p is None else p for p in table]
 
     def line_sends(own, t, got, col):
+        right, left = right_table(t), left_table(t)
+        if t < near and (t == 0 or got[0] is got[1]):
+            tables = [[p if q is None else q for p, q in zip(right, left)]]
+        else:
+            tables = [right, left]
         sends = []
-        for side, table in enumerate((right_table(t), left_table(t))):
+        for side, table in enumerate(tables):
             send = pick(col, filled(table), lambda p: own[p])
             if t > 0:
                 send = (send.astype(F32) + got[side].astype(F32)).astype(BF)
             sends.append(send)
-        return sends
+        return sends if len(sends) == 2 else sends * 2
 
     def line_step(sends, t):
         right = [(z, z + 1) for z in range(nc) if z <= t]
@@ -297,7 +306,7 @@
         return lax.ppermute(sends[0], "col", right), lax.ppermute(sends[1], "col", left)
 
     def line_last(own, got, col):
-        last = pick(col, [position(z, z) for z in range(nc)], lambda p: own[p])
+        last = pick(col, [orders[z].index(z) for z in range(nc)], lambda p: own[p])
         return last.astype(F32) + got[0].astype(F32) + got[1].astype(F32)
 
     def steps(residual, diag_inverse, panels, first_block, probe_solved, genotypes, annotation):
@@ -330,7 +339,7 @@
 
         def partials(load, p, count=2):
             def ids_of(z):
-                return [jnp.where(z < near, nc - 1 - s, s) for s in range(p, p + count)]
+                return [pick(z, [o[s] for o in orders], lambda v: jnp.int32(v)) for s in range(p, p + count)]
 
             return annotate(ids_of, count, row_id, col_id, load[0], load[1], ann, geno, per_slice)
 

time: 173 us -> 171 us (0.988)
  other arithmetic: 11.3 us -> 8.65 us
    convert_element_type x4, other arithmetic: 6.86 us -> 4.34 us  [line_sends(): send = (send.astype(F32) + got[side].astype(F32)).astype(BF)]
  transfers between devices with their start and end apart: 40 -> 40, of which waited for: 19 -> 19; matrix products, arithmetic and copies ran while one was open for 9% -> 8% of each run, Pallas kernels for 11% -> 11%
where the time goes in v3:
time: 171 us; the launch traced here: 168 us
  starting transfers between devices  69.3 us (41%)
  Pallas kernels  43.1 us (25%)
  waiting for transfers between devices  34.3 us (20%)
  other arithmetic  8.65 us (5%)
  matrix products  6.47 us (4%)
  local copies, waits for them, and re-layouts  4.68 us (3%)
  between operations  1.87 us (1%)
    ppermute x30, starting transfers between devices, flip(): return lax.ppermute(x, axis, [(i, i ^ bits) for i in range(size)])  33.2 us
    pallas_call x3, Pallas kernels, annotate(): pl.pallas_call(kernel, grid_spec=pltpu.PrefetchScalarGridSpec(num_scalar_...  33.2 us
    ppermute x4, starting transfers between devices, line_step(): lax.ppermute(sends[0], 'col', right)  27.3 us
    ppermute x30, waiting for transfers between devices, flip(): return lax.ppermute(x, axis, [(i, i ^ bits) for i in range(size)])  25.4 us
    pallas_call x1, Pallas kernels, project(): pl.pallas_call(kernel, grid_spec=pltpu.PrefetchScalarGridSpec(num_scalar_...  8.23 us
    ppermute x2, starting transfers between devices, line_step(): got = lax.ppermute(sends[0], 'col', right + left)  4.78 us
    ppermute x4, waiting for transfers between devices, line_step(): lax.ppermute(sends[0], 'col', right)  4.61 us
    convert_element_type x4, other arithmetic, line_sends(): send = (send.astype(F32) + got[side].astype(F32)).astype(BF)  4.34 us
  transfers between devices with their start and end apart: 40, of which 19 were waited for; matrix products, arithmetic and copies ran while one was open for 8% of the time, Pallas kernels for 11%

profile of v3, /device:TPU:0, one launch (start us, length us, event | category | flops | bytes accessed | tf_op | source)
XLA Modules:
  0.0 168.5 jit_solution(15042354056707514130)
XLA Ops:
  1.3 8.2 %project.1 = (f32[4,8,5120]{2,1,0:T(8,128)}, bf16[4,8,5120]{2,1,0:T(8,128)(2,1)}, f32[4,8,4096]{2,1,0:T(8,128)}, bf16[4,8,4096]{2,1,0:T(8,128)(2,1)}) custom-call(s32[1]{0:T(128)} %copy.29.refs_0_, s32[1]{0:T(128)} %bitcast.3.refs_1_.refs_0_.row_ref, bf16[2048,128]{1,0:T(8,128)(2,1)} %bitcast.126, bf16[2,512,256]{2,1,0:T(8,128)(2,1)} %refs_3_.1, ...), custom_call_target="tpu_custom_call" | custom-call | flops 2147483648 | bytes 16777216 | tf_op jit(solution)/shard_map/project/pallas_call | solution.py:84
  11.7 2.9 %collective-permute-start.1 = (bf16[8,5120]{1,0:T(8,128)(2,1)S(1)}, bf16[8,5120]{1,0:T(8,128)(2,1)S(1)}, u32[]{:S(2)}, u32[]{:S(2)}) collective-permute-start(bf16[8,5120]{1,0:T(8,128)(2,1)S(1)} %get-tuple-element.64), channel_id=1, source_target_pairs={{0,8},{4,12},{8,0},{12,4},{16,24},{20,28},{24,16},{28,20},{1,9},{5... | collective-permute-start | bytes 245768 | tf_op jit(solution)/shard_map/ppermute | solution.py:204
  17.3 2.5 %collective-permute-done.2 = bf16[8,5120]{1,0:T(8,128)(2,1)S(1)} collective-permute-done((bf16[8,5120]{1,0:T(8,128)(2,1)S(1)}, bf16[8,5120]{1,0:T(8,128)(2,1)S(1)}, u32[]{:S(2)}, u32[]{:S(2)}) %collective-permute-start.2) | collective-permute-done | bytes 81952 | tf_op jit(solution)/shard_map/ppermute | solution.py:204
  22.9 2.2 %collective-permute-start.7 = (bf16[8,5120]{1,0:T(8,128)(2,1)S(1)}, bf16[8,5120]{1,0:T(8,128)(2,1)S(1)}, u32[]{:S(2)}, u32[]{:S(2)}) collective-permute-start(bf16[8,5120]{1,0:T(8,128)(2,1)S(1)} %fusion.34), channel_id=1, source_target_pairs={{0,24},{4,28},{8,16},{12,20},{16,8},{20,12},{24,0},{28,4},{1,25},{... | collective-permute-start | bytes 245768 | tf_op jit(solution)/shard_map/ppermute | solution.py:204
  32.4 14.3 %annotate.3 = (bf16[2048,128]{1,0:T(8,128)(2,1)}, bf16[2048,128]{1,0:T(8,128)(2,1)}, bf16[2048,128]{1,0:T(8,128)(2,1)}, bf16[2048,128]{1,0:T(8,128)(2,1)}) custom-call(s32[1]{0:T(128)} %bitcast.3.refs_1_.refs_0_.row_ref, s32[1]{0:T(128)} %bitcast.18.refs_1_, bf16[4,8,5120]{2,1,0:T(8,128)(2,1)} %copy-done, bf16[4,8,5120]{2,1,0:T(8,128)(2,1)} %copy-done.1, ...), custom_call_target="tpu_custom_call" | custom-call | flops 8589934592 | bytes 16777216 | tf_op jit(solution)/shard_map/annotate/pallas_call | solution.py:147
  51.3 2.6 %collective-permute-start.13 = (bf16[256,128]{1,0:T(8,128)(2,1)S(1)}, bf16[256,128]{1,0:T(8,128)(2,1)S(1)}, u32[]{:S(2)}, u32[]{:S(2)}) collective-permute-start(bf16[256,128]{1,0:T(8,128)(2,1)S(1)} %get-tuple-element.79), channel_id=1, source_target_pairs={{0,2},{1,3},{2,0},{3,1},{4,6},{5,7},{6,4},{7,5},{8,10},{9,11},{10,... | collective-permute-start | bytes 196616 | tf_op jit(solution)/shard_map/ppermute | solution.py:204
  57.8 2.1 %collective-permute-done.14 = bf16[256,128]{1,0:T(8,128)(2,1)S(1)} collective-permute-done((bf16[256,128]{1,0:T(8,128)(2,1)S(1)}, bf16[256,128]{1,0:T(8,128)(2,1)S(1)}, u32[]{:S(2)}, u32[]{:S(2)}) %collective-permute-start.14) | collective-permute-done | bytes 65568 | tf_op jit(solution)/shard_map/ppermute | solution.py:204
  66.1 2.5 %collective-permute-start.26 = (bf16[2048,128]{1,0:T(8,128)(2,1)}, bf16[2048,128]{1,0:T(8,128)(2,1)}, u32[]{:S(2)}, u32[]{:S(2)}) collective-permute-start(bf16[2048,128]{1,0:T(8,128)(2,1)} %get-tuple-element.48), channel_id=1, source_target_pairs={{0,1},{3,2},{4,5},{7,6},{8,9},{11,10},{12,13},{15,14},{16,17},{19,... | collective-permute-start | bytes 1572872 | tf_op jit(solution)/shard_map/ppermute | solution.py:304
  70.8 9.4 %annotate.5 = (bf16[2048,128]{1,0:T(8,128)(2,1)}, bf16[2048,128]{1,0:T(8,128)(2,1)}) custom-call(s32[1]{0:T(128)} %bitcast.3.refs_1_.refs_0_.row_ref, s32[1]{0:T(128)} %bitcast.18.refs_1_, bf16[4,8,4096]{2,1,0:T(8,128)(2,1)} %copy-done.4, bf16[4,8,4096]{2,1,0:T(8,128)(2,1)} %copy-done.5, s32[1,4096]{1,0:T(1,128)} %bitcast.133, bf16[2048,4096]{1,0:T(8,128)(2,1)} %bitcast.115), custom_call_target="tpu_custom_call" | custom-call | flops 4294967296 | bytes 16777216 | tf_op jit(solution)/shard_map/annotate/pallas_call | solution.py:147
  80.2 2.3 %collective-permute-start.35 = (bf16[2048,128]{1,0:T(8,128)(2,1)}, bf16[2048,128]{1,0:T(8,128)(2,1)}, u32[]{:S(2)}, u32[]{:S(2)}) collective-permute-start(bf16[2048,128]{1,0:T(8,128)(2,1)} %get-tuple-element.55), channel_id=1, source_target_pairs={{0,1},{3,2},{4,5},{7,6},{8,9},{11,10},{12,13},{15,14},{16,17},{19,... | collective-permute-start | bytes 1572872 | tf_op jit(solution)/shard_map/ppermute | solution.py:304
  82.6 2.1 %fusion.12 = f32[128,6,256]{2,0,1:T(8,128)S(1)} fusion(bf16[2,8,256,512]{3,2,1,0:T(8,128)(2,1)} %param.9, f32[6]{0:T(128)S(1)} %compare_convert_fusion, f32[256,128]{1,0:T(8,128)S(1)} %get-tuple-element.78, f32[256,128]{1,0:T(8,128)S(1)} %get-tuple-element.77), kind=kOutput, calls=%fused_computation.8 | convolution fusion | flops 201785344 | bytes 2621464 | tf_op jit(solution)/shard_map/ngc,cr->ngr/dot_general | solution.py:376
  84.7 2.1 %fusion.18 = bf16[6,256,128]{1,2,0:T(8,128)(2,1)S(1)} fusion(f32[128,6,256]{2,0,1:T(8,128)S(1)} %fusion.12, bf16[2,8,256,512]{3,2,1,0:T(8,128)(2,1)} %param.9, f32[6]{0:T(128)S(1)} %compare_convert_fusion.1, f32[512,128]{1,0:T(8,128)S(1)} %copy-done.3), kind=kOutput, calls=%fused_computation.10 | convolution fusion | flops 201981952 | bytes 3014680 | tf_op jit(solution)/shard_map/ngc,cr->ngr/dot_general | solution.py:374
  87.1 3.7 %collective-permute-start.21 = (bf16[384,128]{1,0:T(8,128)(2,1)S(1)}, bf16[384,128]{1,0:T(8,128)(2,1)S(1)}, u32[]{:S(2)}, u32[]{:S(2)}) collective-permute-start(bf16[384,128]{1,0:T(8,128)(2,1)S(1)} %get-tuple-element.76), channel_id=1, source_target_pairs={{0,2},{1,3},{2,0},{3,1},{4,6},{5,7},{6,4},{7,5},{8,10},{9,11},{10,... | collective-permute-start | bytes 294920 | tf_op jit(solution)/shard_map/ppermute | solution.py:204
  92.3 4.0 %collective-permute-done.20 = bf16[384,128]{1,0:T(8,128)(2,1)S(1)} collective-permute-done((bf16[384,128]{1,0:T(8,128)(2,1)S(1)}, bf16[384,128]{1,0:T(8,128)(2,1)S(1)}, u32[]{:S(2)}, u32[]{:S(2)}) %collective-permute-start.20) | collective-permute-done | bytes 98336 | tf_op jit(solution)/shard_map/ppermute | solution.py:204
  96.4 2.1 %collective-permute-done.21 = bf16[384,128]{1,0:T(8,128)(2,1)S(1)} collective-permute-done((bf16[384,128]{1,0:T(8,128)(2,1)S(1)}, bf16[384,128]{1,0:T(8,128)(2,1)S(1)}, u32[]{:S(2)}, u32[]{:S(2)}) %collective-permute-start.21) | collective-permute-done | bytes 98336 | tf_op jit(solution)/shard_map/ppermute | solution.py:204
  98.5 5.3 %collective-permute-done.22 = bf16[384,128]{1,0:T(8,128)(2,1)S(1)} collective-permute-done((bf16[384,128]{1,0:T(8,128)(2,1)S(1)}, bf16[384,128]{1,0:T(8,128)(2,1)S(1)}, u32[]{:S(2)}, u32[]{:S(2)}) %collective-permute-start.22) | collective-permute-done | bytes 98336 | tf_op jit(solution)/shard_map/ppermute | solution.py:204
  104.7 3.6 %collective-permute-start.25 = (bf16[384,128]{1,0:T(8,128)(2,1)S(1)}, bf16[384,128]{1,0:T(8,128)(2,1)S(1)}, u32[]{:S(2)}, u32[]{:S(2)}) collective-permute-start(bf16[384,128]{1,0:T(8,128)(2,1)S(1)} %fusion.30), channel_id=1, source_target_pairs={{0,1},{1,0},{2,3},{3,2},{4,5},{5,4},{6,7},{7,6},{8,9},{9,8},{10,11... | collective-permute-start | bytes 294920 | tf_op jit(solution)/shard_map/ppermute | solution.py:204
  109.4 2.7 %collective-permute-start.27 = (bf16[2048,128]{1,0:T(8,128)(2,1)S(1)}, bf16[2048,128]{1,0:T(8,128)(2,1)}, u32[]{:S(2)}, u32[]{:S(2)}) collective-permute-start(bf16[2048,128]{1,0:T(8,128)(2,1)S(1)} %add_convert_fusion.7), channel_id=1, source_target_pairs={{0,1},{1,2},{4,5},{5,6},{8,9},{9,10},{12,13},{13,14},{16,17},{17,1... | collective-permute-start | bytes 1572872 | tf_op jit(solution)/shard_map/ppermute | solution.py:306
  112.2 9.4 %annotate.4 = (bf16[2048,128]{1,0:T(8,128)(2,1)}, bf16[2048,128]{1,0:T(8,128)(2,1)}) custom-call(s32[1]{0:T(128)} %bitcast.3.refs_1_.refs_0_.row_ref, s32[1]{0:T(128)} %bitcast.18.refs_1_, bf16[4,8,4096]{2,1,0:T(8,128)(2,1)} %copy-done.4, bf16[4,8,4096]{2,1,0:T(8,128)(2,1)} %copy-done.5, s32[1,4096]{1,0:T(1,128)} %bitcast.134, bf16[2048,4096]{1,0:T(8,128)(2,1)} %bitcast.116), custom_call_target="tpu_custom_call" | custom-call | flops 4294967296 | bytes 16777216 | tf_op jit(solution)/shard_map/annotate/pallas_call | solution.py:147
  124.0 2.3 %collective-permute-start.36 = (bf16[2048,128]{1,0:T(8,128)(2,1)S(1)}, bf16[2048,128]{1,0:T(8,128)(2,1)S(1)}, u32[]{:S(2)}, u32[]{:S(2)}) collective-permute-start(bf16[2048,128]{1,0:T(8,128)(2,1)S(1)} %add_convert_fusion.3), channel_id=1, source_target_pairs={{0,1},{1,2},{4,5},{5,6},{8,9},{9,10},{12,13},{13,14},{16,17},{17,1... | collective-permute-start | bytes 1572872 | tf_op jit(solution)/shard_map/ppermute | solution.py:306
  128.6 13.3 %collective-permute-start.28 = (bf16[2048,128]{1,0:T(8,128)(2,1)S(1)}, bf16[2048,128]{1,0:T(8,128)(2,1)S(1)}, u32[]{:S(2)}, u32[]{:S(2)}) collective-permute-start(bf16[2048,128]{1,0:T(8,128)(2,1)S(1)} %get-tuple-element.60), channel_id=1, source_target_pairs={{0,1},{1,2},{2,3},{4,5},{5,6},{6,7},{8,9},{9,10},{10,11},{12,13},{... | collective-permute-start | bytes 1572872 | tf_op jit(solution)/shard_map/ppermute | solution.py:306
  143.5 9.0 %collective-permute-start.37 = (bf16[2048,128]{1,0:T(8,128)(2,1)S(1)}, bf16[2048,128]{1,0:T(8,128)(2,1)}, u32[]{:S(2)}, u32[]{:S(2)}) collective-permute-start(bf16[2048,128]{1,0:T(8,128)(2,1)S(1)} %get-tuple-element.62), channel_id=1, source_target_pairs={{0,1},{1,2},{2,3},{4,5},{5,6},{6,7},{8,9},{9,10},{10,11},{12,13},{... | collective-permute-start | bytes 1572872 | tf_op jit(solution)/shard_map/ppermute | solution.py:306
  155.5 4.6 %collective-permute-done.37 = bf16[2048,128]{1,0:T(8,128)(2,1)} collective-permute-done((bf16[2048,128]{1,0:T(8,128)(2,1)S(1)}, bf16[2048,128]{1,0:T(8,128)(2,1)}, u32[]{:S(2)}, u32[]{:S(2)}) %collective-permute-start.37) | collective-permute-done | bytes 524320 | tf_op jit(solution)/shard_map/ppermute | solution.py:306
  160.1 4.3 %collective-permute-done.39 = bf16[2048,128]{1,0:T(8,128)(2,1)} collective-permute-done((bf16[2048,128]{1,0:T(8,128)(2,1)S(1)}, bf16[2048,128]{1,0:T(8,128)(2,1)}, u32[]{:S(2)}, u32[]{:S(2)}) %collective-permute-start.39) | collective-permute-done | bytes 524320 | tf_op jit(solution)/shard_map/ppermute | solution.py:306
  (139 shorter events, 49.1 us)
Async XLA Ops:
  10.1 11.4 %collective-permute-start.4 = (bf16[4,8,4096]{2,1,0:T(8,128)(2,1)}, bf16[4,8,4096]{2,1,0:T(8,128)(2,1)S(1)}, u32[]{:S(2)}, u32[]{:S(2)}) collective-permute-start(bf16[4,8,4096]{2,1,0:T(8,128)(2,1)} %get-tuple-element.32), channel_id=1, source_target_pairs={{0,4},{4,0},{8,12},{12,8},{16,20},{20,16},{24,28},{28,24},{1,5},{5... | collective-permute-start | bytes 786440 | tf_op jit(solution)/shard_map/ppermute | solution.py:204
  22.1 6.8 %collective-permute-start.6 = (bf16[8,5120]{1,0:T(8,128)(2,1)S(1)}, bf16[8,5120]{1,0:T(8,128)(2,1)S(1)}, u32[]{:S(2)}, u32[]{:S(2)}) collective-permute-start(bf16[8,5120]{1,0:T(8,128)(2,1)S(1)} %fusion.34), channel_id=1, source_target_pairs={{0,16},{4,20},{8,24},{12,28},{16,0},{20,4},{24,8},{28,12},{1,17},{... | collective-permute-start | bytes 245768 | tf_op jit(solution)/shard_map/ppermute | solution.py:204
  49.6 6.6 %collective-permute-start.12 = (bf16[256,128]{1,0:T(8,128)(2,1)S(1)}, bf16[256,128]{1,0:T(8,128)(2,1)S(1)}, u32[]{:S(2)}, u32[]{:S(2)}) collective-permute-start(bf16[256,128]{1,0:T(8,128)(2,1)S(1)} %get-tuple-element.79), channel_id=1, source_target_pairs={{0,1},{1,0},{2,3},{3,2},{4,5},{5,4},{6,7},{7,6},{8,9},{9,8},{10,11... | collective-permute-start | bytes 196616 | tf_op jit(solution)/shard_map/ppermute | solution.py:204
  51.3 6.6 %collective-permute-start.13 = (bf16[256,128]{1,0:T(8,128)(2,1)S(1)}, bf16[256,128]{1,0:T(8,128)(2,1)S(1)}, u32[]{:S(2)}, u32[]{:S(2)}) collective-permute-start(bf16[256,128]{1,0:T(8,128)(2,1)S(1)} %get-tuple-element.79), channel_id=1, source_target_pairs={{0,2},{1,3},{2,0},{3,1},{4,6},{5,7},{6,4},{7,5},{8,10},{9,11},{10,... | collective-permute-start | bytes 196616 | tf_op jit(solution)/shard_map/ppermute | solution.py:204
  53.9 6.1 %collective-permute-start.14 = (bf16[256,128]{1,0:T(8,128)(2,1)S(1)}, bf16[256,128]{1,0:T(8,128)(2,1)S(1)}, u32[]{:S(2)}, u32[]{:S(2)}) collective-permute-start(bf16[256,128]{1,0:T(8,128)(2,1)S(1)} %get-tuple-element.79), channel_id=1, source_target_pairs={{0,3},{1,2},{2,1},{3,0},{4,7},{5,6},{6,5},{7,4},{8,11},{9,10},{10,... | collective-permute-start | bytes 196616 | tf_op jit(solution)/shard_map/ppermute | solution.py:204
  54.1 7.2 %collective-permute-start.31 = (bf16[8,4096]{1,0:T(8,128)(2,1)S(1)}, bf16[8,4096]{1,0:T(8,128)(2,1)S(1)}, u32[]{:S(2)}, u32[]{:S(2)}) collective-permute-start(bf16[8,4096]{1,0:T(8,128)(2,1)S(1)} %fusion.41), channel_id=1, source_target_pairs={{0,8},{4,12},{8,0},{12,4},{16,24},{20,28},{24,16},{28,20},{1,9},{5... | collective-permute-start | bytes 196616 | tf_op jit(solution)/shard_map/ppermute | solution.py:204
  61.5 8.6 %collective-permute-start.34 = (bf16[4,8,4096]{2,1,0:T(8,128)(2,1)S(1)}, bf16[4,8,4096]{2,1,0:T(8,128)(2,1)S(1)}, u32[]{:S(2)}, u32[]{:S(2)}) collective-permute-start(bf16[4,8,4096]{2,1,0:T(8,128)(2,1)S(1)} %pad_maximum_fusion.4.refs_2_), channel_id=1, source_target_pairs={{0,4},{4,0},{8,12},{12,8},{16,20},{20,16},{24,28},{28,24},{1,5},{5... | collective-permute-start | bytes 786440 | tf_op jit(solution)/shard_map/ppermute | solution.py:204
  62.5 6.0 %collective-permute-start.16 = (bf16[256,128]{1,0:T(8,128)(2,1)S(1)}, bf16[256,128]{1,0:T(8,128)(2,1)S(1)}, u32[]{:S(2)}, u32[]{:S(2)}) collective-permute-start(bf16[256,128]{1,0:T(8,128)(2,1)S(1)} %fusion.54), channel_id=1, source_target_pairs={{0,8},{4,12},{8,0},{12,4},{16,24},{20,28},{24,16},{28,20},{1,9},{5... | collective-permute-start | bytes 196616 | tf_op jit(solution)/shard_map/ppermute | solution.py:204
  66.1 42.2 %collective-permute-start.26 = (bf16[2048,128]{1,0:T(8,128)(2,1)}, bf16[2048,128]{1,0:T(8,128)(2,1)}, u32[]{:S(2)}, u32[]{:S(2)}) collective-permute-start(bf16[2048,128]{1,0:T(8,128)(2,1)} %get-tuple-element.48), channel_id=1, source_target_pairs={{0,1},{3,2},{4,5},{7,6},{8,9},{11,10},{12,13},{15,14},{16,17},{19,... | collective-permute-start | bytes 1572872 | tf_op jit(solution)/shard_map/ppermute | solution.py:304
  70.0 12.6 %collective-permute-start.19 = (f32[256,128]{1,0:T(8,128)S(1)}, f32[256,128]{1,0:T(8,128)S(1)}, u32[]{:S(2)}, u32[]{:S(2)}) collective-permute-start(f32[256,128]{1,0:T(8,128)S(1)} %convert_add_fusion.3), channel_id=1, source_target_pairs={{0,4},{4,0},{8,12},{12,8},{16,20},{20,16},{24,28},{28,24},{1,5},{5... | collective-permute-start | bytes 393224 | tf_op jit(solution)/shard_map/ppermute | solution.py:204
  80.2 42.4 %collective-permute-start.35 = (bf16[2048,128]{1,0:T(8,128)(2,1)}, bf16[2048,128]{1,0:T(8,128)(2,1)}, u32[]{:S(2)}, u32[]{:S(2)}) collective-permute-start(bf16[2048,128]{1,0:T(8,128)(2,1)} %get-tuple-element.55), channel_id=1, source_target_pairs={{0,1},{3,2},{4,5},{7,6},{8,9},{11,10},{12,13},{15,14},{16,17},{19,... | collective-permute-start | bytes 1572872 | tf_op jit(solution)/shard_map/ppermute | solution.py:304
  87.0 9.4 %collective-permute-start.20 = (bf16[384,128]{1,0:T(8,128)(2,1)S(1)}, bf16[384,128]{1,0:T(8,128)(2,1)S(1)}, u32[]{:S(2)}, u32[]{:S(2)}) collective-permute-start(bf16[384,128]{1,0:T(8,128)(2,1)S(1)} %get-tuple-element.74), channel_id=1, source_target_pairs={{0,1},{1,0},{2,3},{3,2},{4,5},{5,4},{6,7},{7,6},{8,9},{9,8},{10,11... | collective-permute-start | bytes 294920 | tf_op jit(solution)/shard_map/ppermute | solution.py:204
  87.1 11.4 %collective-permute-start.21 = (bf16[384,128]{1,0:T(8,128)(2,1)S(1)}, bf16[384,128]{1,0:T(8,128)(2,1)S(1)}, u32[]{:S(2)}, u32[]{:S(2)}) collective-permute-start(bf16[384,128]{1,0:T(8,128)(2,1)S(1)} %get-tuple-element.76), channel_id=1, source_target_pairs={{0,2},{1,3},{2,0},{3,1},{4,6},{5,7},{6,4},{7,5},{8,10},{9,11},{10,... | collective-permute-start | bytes 294920 | tf_op jit(solution)/shard_map/ppermute | solution.py:204
  90.8 12.9 %collective-permute-start.22 = (bf16[384,128]{1,0:T(8,128)(2,1)S(1)}, bf16[384,128]{1,0:T(8,128)(2,1)S(1)}, u32[]{:S(2)}, u32[]{:S(2)}) collective-permute-start(bf16[384,128]{1,0:T(8,128)(2,1)S(1)} %get-tuple-element.75), channel_id=1, source_target_pairs={{0,3},{1,2},{2,1},{3,0},{4,7},{5,6},{6,5},{7,4},{8,11},{9,10},{10,... | collective-permute-start | bytes 294920 | tf_op jit(solution)/shard_map/ppermute | solution.py:204
  103.8 17.8 %collective-permute-start.23 = (bf16[384,128]{1,0:T(8,128)(2,1)S(1)}, bf16[384,128]{1,0:T(8,128)(2,1)S(1)}, u32[]{:S(2)}, u32[]{:S(2)}) collective-permute-start(bf16[384,128]{1,0:T(8,128)(2,1)S(1)} %fusion.30), channel_id=1, source_target_pairs={{0,3},{1,2},{2,1},{3,0},{4,7},{5,6},{6,5},{7,4},{8,11},{9,10},{10,... | collective-permute-start | bytes 294920 | tf_op jit(solution)/shard_map/ppermute | solution.py:204
  104.7 17.8 %collective-permute-start.24 = (bf16[384,128]{1,0:T(8,128)(2,1)S(1)}, bf16[384,128]{1,0:T(8,128)(2,1)S(1)}, u32[]{:S(2)}, u32[]{:S(2)}) collective-permute-start(bf16[384,128]{1,0:T(8,128)(2,1)S(1)} %fusion.30), channel_id=1, source_target_pairs={{0,2},{1,3},{2,0},{3,1},{4,6},{5,7},{6,4},{7,5},{8,10},{9,11},{10,... | collective-permute-start | bytes 294920 | tf_op jit(solution)/shard_map/ppermute | solution.py:204
  104.7 17.8 %collective-permute-start.25 = (bf16[384,128]{1,0:T(8,128)(2,1)S(1)}, bf16[384,128]{1,0:T(8,128)(2,1)S(1)}, u32[]{:S(2)}, u32[]{:S(2)}) collective-permute-start(bf16[384,128]{1,0:T(8,128)(2,1)S(1)} %fusion.30), channel_id=1, source_target_pairs={{0,1},{1,0},{2,3},{3,2},{4,5},{5,4},{6,7},{7,6},{8,9},{9,8},{10,11... | collective-permute-start | bytes 294920 | tf_op jit(solution)/shard_map/ppermute | solution.py:204
  109.4 17.6 %collective-permute-start.27 = (bf16[2048,128]{1,0:T(8,128)(2,1)S(1)}, bf16[2048,128]{1,0:T(8,128)(2,1)}, u32[]{:S(2)}, u32[]{:S(2)}) collective-permute-start(bf16[2048,128]{1,0:T(8,128)(2,1)S(1)} %add_convert_fusion.7), channel_id=1, source_target_pairs={{0,1},{1,2},{4,5},{5,6},{8,9},{9,10},{12,13},{13,14},{16,17},{17,1... | collective-permute-start | bytes 1572872 | tf_op jit(solution)/shard_map/ppermute | solution.py:306
  124.0 19.2 %collective-permute-start.36 = (bf16[2048,128]{1,0:T(8,128)(2,1)S(1)}, bf16[2048,128]{1,0:T(8,128)(2,1)S(1)}, u32[]{:S(2)}, u32[]{:S(2)}) collective-permute-start(bf16[2048,128]{1,0:T(8,128)(2,1)S(1)} %add_convert_fusion.3), channel_id=1, source_target_pairs={{0,1},{1,2},{4,5},{5,6},{8,9},{9,10},{12,13},{13,14},{16,17},{17,1... | collective-permute-start | bytes 1572872 | tf_op jit(solution)/shard_map/ppermute | solution.py:306
  126.3 16.9 %collective-permute-start.38 = (bf16[2048,128]{1,0:T(8,128)(2,1)S(1)}, bf16[2048,128]{1,0:T(8,128)(2,1)S(1)}, u32[]{:S(2)}, u32[]{:S(2)}) collective-permute-start(bf16[2048,128]{1,0:T(8,128)(2,1)S(1)} %add_convert_fusion.3), channel_id=1, source_target_pairs={{2,1},{3,2},{6,5},{7,6},{10,9},{11,10},{14,13},{15,14},{18,17},{19... | collective-permute-start | bytes 1572872 | tf_op jit(solution)/shard_map/ppermute | solution.py:306
  128.6 26.4 %collective-permute-start.28 = (bf16[2048,128]{1,0:T(8,128)(2,1)S(1)}, bf16[2048,128]{1,0:T(8,128)(2,1)S(1)}, u32[]{:S(2)}, u32[]{:S(2)}) collective-permute-start(bf16[2048,128]{1,0:T(8,128)(2,1)S(1)} %get-tuple-element.60), channel_id=1, source_target_pairs={{0,1},{1,2},{2,3},{4,5},{5,6},{6,7},{8,9},{9,10},{10,11},{12,13},{... | collective-permute-start | bytes 1572872 | tf_op jit(solution)/shard_map/ppermute | solution.py:306
  141.8 13.1 %collective-permute-start.30 = (bf16[2048,128]{1,0:T(8,128)(2,1)S(1)}, bf16[2048,128]{1,0:T(8,128)(2,1)S(1)}, u32[]{:S(2)}, u32[]{:S(2)}) collective-permute-start(bf16[2048,128]{1,0:T(8,128)(2,1)S(1)} %get-tuple-element.61), channel_id=1, source_target_pairs={{1,0},{2,1},{3,2},{5,4},{6,5},{7,6},{9,8},{10,9},{11,10},{13,12},{... | collective-permute-start | bytes 1572872 | tf_op jit(solution)/shard_map/ppermute | solution.py:306
  143.5 16.6 %collective-permute-start.37 = (bf16[2048,128]{1,0:T(8,128)(2,1)S(1)}, bf16[2048,128]{1,0:T(8,128)(2,1)}, u32[]{:S(2)}, u32[]{:S(2)}) collective-permute-start(bf16[2048,128]{1,0:T(8,128)(2,1)S(1)} %get-tuple-element.62), channel_id=1, source_target_pairs={{0,1},{1,2},{2,3},{4,5},{5,6},{6,7},{8,9},{9,10},{10,11},{12,13},{... | collective-permute-start | bytes 1572872 | tf_op jit(solution)/shard_map/ppermute | solution.py:306
  152.5 11.8 %collective-permute-start.39 = (bf16[2048,128]{1,0:T(8,128)(2,1)S(1)}, bf16[2048,128]{1,0:T(8,128)(2,1)}, u32[]{:S(2)}, u32[]{:S(2)}) collective-permute-start(bf16[2048,128]{1,0:T(8,128)(2,1)S(1)} %get-tuple-element.63), channel_id=1, source_target_pairs={{1,0},{2,1},{3,2},{5,4},{6,5},{7,6},{9,8},{10,9},{11,10},{13,12},{... | collective-permute-start | bytes 1572872 | tf_op jit(solution)/shard_map/ppermute | solution.py:306
  (33 other events, 237.6 us)

commit v4 on v3

--- a/solution.py
+++ b/solution.py
@@ -139,7 +139,7 @@
     chips, part, _ = mine.shape
     width = 2 * chips * part
     wide = per_slice * width
-    tile = rows // 2
+    tile = rows // 4
 
     def kernel(*refs):
         annotate_kernel(ids_of, slices, per_slice, *refs)
@@ -350,14 +350,11 @@
         solved_load, own0 = barrier((load0, own0))
         first = unfold(row_id, solved_load[0], solved_load[1], snps, rhs)
         first_bf = first.astype(BF)
-        own1 = partials(load1, 0)
+        own1 = partials(load1, 0, nc)
         got1 = line_step(line_sends(own1, 0, None, col), 0)
         for t in range(1, nc - 1):
             sends = line_sends(own0, t, got0, col)
             got0 = line_step(sends, t)
-            if 2 * t < nc:
-                load1, sends = barrier((load1, sends))
-                own1 = own1 + partials(load1, 2 * t)
             got1 = line_step(line_sends(own1, t, got1, col), t)
         summed = [line_last(own0, got0, col), line_last(own1, got1, col)]
 

time: 171 us -> 165 us (0.965)
  waiting for transfers between devices: 34.3 us -> 44.3 us
  starting transfers between devices: 69.3 us -> 60.4 us
  Pallas kernels: 43.1 us -> 36.8 us
    ppermute x4, waiting for transfers between devices: 4.61 us -> 17.2 us  [line_step(): lax.ppermute(sends[0], 'col', right)]
    ppermute x4, starting transfers between devices: 27.3 us -> 18.5 us  [line_step(): lax.ppermute(sends[0], 'col', right)]
    pallas_call x3 -> x2, Pallas kernels: 33.2 us -> 26.8 us  [annotate(): pl.pallas_call(kernel, grid_spec=pltpu.PrefetchScalarGridSpec(num_scalar_...]
    ppermute x4, waiting for transfers between devices: 4.26 us -> 0.01 us  [line_step(): lax.ppermute(sends[1], 'col', left)]
  transfers between devices with their start and end apart: 40 -> 40, of which waited for: 19 -> 22; matrix products, arithmetic and copies ran while one was open for 8% -> 8% of each run, Pallas kernels for 11% -> 8%
where the time goes in v4:
time: 165 us; the launch traced here: 163 us
  starting transfers between devices  60.4 us (37%)
  waiting for transfers between devices  44.3 us (27%)
  Pallas kernels  36.8 us (22%)
  other arithmetic  8.49 us (5%)
  matrix products  6.47 us (4%)
  local copies, waits for them, and re-layouts  4.69 us (3%)
  between operations  1.8 us (1%)
    ppermute x30, starting transfers between devices, flip(): return lax.ppermute(x, axis, [(i, i ^ bits) for i in range(size)])  33.2 us
    ppermute x30, waiting for transfers between devices, flip(): return lax.ppermute(x, axis, [(i, i ^ bits) for i in range(size)])  27.1 us
    pallas_call x2, Pallas kernels, annotate(): pl.pallas_call(kernel, grid_spec=pltpu.PrefetchScalarGridSpec(num_scalar_...  26.8 us
    ppermute x4, starting transfers between devices, line_step(): lax.ppermute(sends[0], 'col', right)  18.5 us
    ppermute x4, waiting for transfers between devices, line_step(): lax.ppermute(sends[0], 'col', right)  17.2 us
    pallas_call x1, Pallas kernels, project(): pl.pallas_call(kernel, grid_spec=pltpu.PrefetchScalarGridSpec(num_scalar_...  8.22 us
    ppermute x2, starting transfers between devices, line_step(): got = lax.ppermute(sends[0], 'col', right + left)  4.84 us
    convert_element_type x4, other arithmetic, line_sends(): send = (send.astype(F32) + got[side].astype(F32)).astype(BF)  4.18 us
  transfers between devices with their start and end apart: 40, of which 22 were waited for; matrix products, arithmetic and copies ran while one was open for 8% of the time, Pallas kernels for 8%

profile of v4, /device:TPU:0, one launch (start us, length us, event | category | flops | bytes accessed | tf_op | source)
XLA Modules:
  0.0 163.0 jit_solution(12331145055532355212)
XLA Ops:
  1.3 8.2 %project.1 = (f32[4,8,5120]{2,1,0:T(8,128)}, bf16[4,8,5120]{2,1,0:T(8,128)(2,1)}, f32[4,8,4096]{2,1,0:T(8,128)}, bf16[4,8,4096]{2,1,0:T(8,128)(2,1)}) custom-call(s32[1]{0:T(128)} %copy.29.refs_0_, s32[1]{0:T(128)} %bitcast.3.refs_1_.refs_0_.row_ref, bf16[2048,128]{1,0:T(8,128)(2,1)} %bitcast.125, bf16[2,512,256]{2,1,0:T(8,128)(2,1)} %refs_3_.1, ...), custom_call_target="tpu_custom_call" | custom-call | flops 2147483648 | bytes 16777216 | tf_op jit(solution)/shard_map/project/pallas_call | solution.py:84
  11.6 2.9 %collective-permute-start.1 = (bf16[8,5120]{1,0:T(8,128)(2,1)S(1)}, bf16[8,5120]{1,0:T(8,128)(2,1)S(1)}, u32[]{:S(2)}, u32[]{:S(2)}) collective-permute-start(bf16[8,5120]{1,0:T(8,128)(2,1)S(1)} %get-tuple-element.60), channel_id=1, source_target_pairs={{0,8},{4,12},{8,0},{12,4},{16,24},{20,28},{24,16},{28,20},{1,9},{5... | collective-permute-start | bytes 245768 | tf_op jit(solution)/shard_map/ppermute | solution.py:204
  17.3 2.5 %collective-permute-done.2 = bf16[8,5120]{1,0:T(8,128)(2,1)S(1)} collective-permute-done((bf16[8,5120]{1,0:T(8,128)(2,1)S(1)}, bf16[8,5120]{1,0:T(8,128)(2,1)S(1)}, u32[]{:S(2)}, u32[]{:S(2)}) %collective-permute-start.2) | collective-permute-done | bytes 81952 | tf_op jit(solution)/shard_map/ppermute | solution.py:204
  22.9 2.2 %collective-permute-start.7 = (bf16[8,5120]{1,0:T(8,128)(2,1)S(1)}, bf16[8,5120]{1,0:T(8,128)(2,1)S(1)}, u32[]{:S(2)}, u32[]{:S(2)}) collective-permute-start(bf16[8,5120]{1,0:T(8,128)(2,1)S(1)} %fusion.34), channel_id=1, source_target_pairs={{0,24},{4,28},{8,16},{12,20},{16,8},{20,12},{24,0},{28,4},{1,25},{... | collective-permute-start | bytes 245768 | tf_op jit(solution)/shard_map/ppermute | solution.py:204
  32.4 13.4 %annotate.2 = (bf16[2048,128]{1,0:T(8,128)(2,1)}, bf16[2048,128]{1,0:T(8,128)(2,1)}, bf16[2048,128]{1,0:T(8,128)(2,1)}, bf16[2048,128]{1,0:T(8,128)(2,1)}) custom-call(s32[1]{0:T(128)} %bitcast.3.refs_1_.refs_0_.row_ref, s32[1]{0:T(128)} %bitcast.18.refs_1_, bf16[4,8,5120]{2,1,0:T(8,128)(2,1)} %copy-done, bf16[4,8,5120]{2,1,0:T(8,128)(2,1)} %copy-done.1, ...), custom_call_target="tpu_custom_call" | custom-call | flops 8589934592 | bytes 16777216 | tf_op jit(solution)/shard_map/annotate/pallas_call | solution.py:147
  50.4 2.6 %collective-permute-start.13 = (bf16[256,128]{1,0:T(8,128)(2,1)S(1)}, bf16[256,128]{1,0:T(8,128)(2,1)S(1)}, u32[]{:S(2)}, u32[]{:S(2)}) collective-permute-start(bf16[256,128]{1,0:T(8,128)(2,1)S(1)} %get-tuple-element.75), channel_id=1, source_target_pairs={{0,2},{1,3},{2,0},{3,1},{4,6},{5,7},{6,4},{7,5},{8,10},{9,11},{10,... | collective-permute-start | bytes 196616 | tf_op jit(solution)/shard_map/ppermute | solution.py:204
  56.9 2.1 %collective-permute-done.14 = bf16[256,128]{1,0:T(8,128)(2,1)S(1)} collective-permute-done((bf16[256,128]{1,0:T(8,128)(2,1)S(1)}, bf16[256,128]{1,0:T(8,128)(2,1)S(1)}, u32[]{:S(2)}, u32[]{:S(2)}) %collective-permute-start.14) | collective-permute-done | bytes 65568 | tf_op jit(solution)/shard_map/ppermute | solution.py:204
  65.2 2.5 %collective-permute-start.26 = (bf16[2048,128]{1,0:T(8,128)(2,1)}, bf16[2048,128]{1,0:T(8,128)(2,1)}, u32[]{:S(2)}, u32[]{:S(2)}) collective-permute-start(bf16[2048,128]{1,0:T(8,128)(2,1)} %get-tuple-element.46), channel_id=1, source_target_pairs={{0,1},{3,2},{4,5},{7,6},{8,9},{11,10},{12,13},{15,14},{16,17},{19,... | collective-permute-start | bytes 1572872 | tf_op jit(solution)/shard_map/ppermute | solution.py:304
  69.9 13.4 %annotate.3 = (bf16[2048,128]{1,0:T(8,128)(2,1)}, bf16[2048,128]{1,0:T(8,128)(2,1)}, bf16[2048,128]{1,0:T(8,128)(2,1)}, bf16[2048,128]{1,0:T(8,128)(2,1)}) custom-call(s32[1]{0:T(128)} %bitcast.3.refs_1_.refs_0_.row_ref, s32[1]{0:T(128)} %bitcast.18.refs_1_, bf16[4,8,4096]{2,1,0:T(8,128)(2,1)} %copy-done.13, bf16[4,8,4096]{2,1,0:T(8,128)(2,1)} %copy-done.14, ...), custom_call_target="tpu_custom_call" | custom-call | flops 8589934592 | bytes 16777216 | tf_op jit(solution)/shard_map/annotate/pallas_call | solution.py:147
  83.3 2.3 %collective-permute-start.35 = (bf16[2048,128]{1,0:T(8,128)(2,1)}, bf16[2048,128]{1,0:T(8,128)(2,1)}, u32[]{:S(2)}, u32[]{:S(2)}) collective-permute-start(bf16[2048,128]{1,0:T(8,128)(2,1)} %get-tuple-element.51), channel_id=1, source_target_pairs={{0,1},{3,2},{4,5},{7,6},{8,9},{11,10},{12,13},{15,14},{16,17},{19,... | collective-permute-start | bytes 1572872 | tf_op jit(solution)/shard_map/ppermute | solution.py:304
  85.7 2.1 %fusion.12 = f32[128,6,256]{2,0,1:T(8,128)S(1)} fusion(bf16[2,8,256,512]{3,2,1,0:T(8,128)(2,1)} %param.9, f32[6]{0:T(128)S(1)} %compare_convert_fusion, f32[256,128]{1,0:T(8,128)S(1)} %get-tuple-element.74, f32[256,128]{1,0:T(8,128)S(1)} %get-tuple-element.73), kind=kOutput, calls=%fused_computation.8 | convolution fusion | flops 201785344 | bytes 2621464 | tf_op jit(solution)/shard_map/ngc,cr->ngr/dot_general | solution.py:373
  87.8 2.1 %fusion.18 = bf16[6,256,128]{1,2,0:T(8,128)(2,1)S(1)} fusion(f32[128,6,256]{2,0,1:T(8,128)S(1)} %fusion.12, bf16[2,8,256,512]{3,2,1,0:T(8,128)(2,1)} %param.9, f32[6]{0:T(128)S(1)} %compare_convert_fusion.1, f32[512,128]{1,0:T(8,128)S(1)} %copy-done.3), kind=kOutput, calls=%fused_computation.10 | convolution fusion | flops 201981952 | bytes 3014680 | tf_op jit(solution)/shard_map/ngc,cr->ngr/dot_general | solution.py:371
  90.2 3.7 %collective-permute-start.21 = (bf16[384,128]{1,0:T(8,128)(2,1)S(1)}, bf16[384,128]{1,0:T(8,128)(2,1)S(1)}, u32[]{:S(2)}, u32[]{:S(2)}) collective-permute-start(bf16[384,128]{1,0:T(8,128)(2,1)S(1)} %get-tuple-element.72), channel_id=1, source_target_pairs={{0,2},{1,3},{2,0},{3,1},{4,6},{5,7},{6,4},{7,5},{8,10},{9,11},{10,... | collective-permute-start | bytes 294920 | tf_op jit(solution)/shard_map/ppermute | solution.py:204
  95.4 4.0 %collective-permute-done.20 = bf16[384,128]{1,0:T(8,128)(2,1)S(1)} collective-permute-done((bf16[384,128]{1,0:T(8,128)(2,1)S(1)}, bf16[384,128]{1,0:T(8,128)(2,1)S(1)}, u32[]{:S(2)}, u32[]{:S(2)}) %collective-permute-start.20) | collective-permute-done | bytes 98336 | tf_op jit(solution)/shard_map/ppermute | solution.py:204
  99.5 2.1 %collective-permute-done.21 = bf16[384,128]{1,0:T(8,128)(2,1)S(1)} collective-permute-done((bf16[384,128]{1,0:T(8,128)(2,1)S(1)}, bf16[384,128]{1,0:T(8,128)(2,1)S(1)}, u32[]{:S(2)}, u32[]{:S(2)}) %collective-permute-start.21) | collective-permute-done | bytes 98336 | tf_op jit(solution)/shard_map/ppermute | solution.py:204
  101.6 5.2 %collective-permute-done.22 = bf16[384,128]{1,0:T(8,128)(2,1)S(1)} collective-permute-done((bf16[384,128]{1,0:T(8,128)(2,1)S(1)}, bf16[384,128]{1,0:T(8,128)(2,1)S(1)}, u32[]{:S(2)}, u32[]{:S(2)}) %collective-permute-start.22) | collective-permute-done | bytes 98336 | tf_op jit(solution)/shard_map/ppermute | solution.py:204
  107.8 3.6 %collective-permute-start.25 = (bf16[384,128]{1,0:T(8,128)(2,1)S(1)}, bf16[384,128]{1,0:T(8,128)(2,1)S(1)}, u32[]{:S(2)}, u32[]{:S(2)}) collective-permute-start(bf16[384,128]{1,0:T(8,128)(2,1)S(1)} %fusion.30), channel_id=1, source_target_pairs={{0,1},{1,0},{2,3},{3,2},{4,5},{5,4},{6,7},{7,6},{8,9},{9,8},{10,11... | collective-permute-start | bytes 294920 | tf_op jit(solution)/shard_map/ppermute | solution.py:204
  112.6 2.1 %collective-permute-start.27 = (bf16[2048,128]{1,0:T(8,128)(2,1)S(1)}, bf16[2048,128]{1,0:T(8,128)(2,1)S(1)}, u32[]{:S(2)}, u32[]{:S(2)}) collective-permute-start(bf16[2048,128]{1,0:T(8,128)(2,1)S(1)} %add_convert_fusion.7), channel_id=1, source_target_pairs={{0,1},{1,2},{4,5},{5,6},{8,9},{9,10},{12,13},{13,14},{16,17},{17,1... | collective-permute-start | bytes 1572872 | tf_op jit(solution)/shard_map/ppermute | solution.py:306
  115.3 1.7 %collective-permute-done.24 = bf16[384,128]{1,0:T(8,128)(2,1)S(1)} collective-permute-done((bf16[384,128]{1,0:T(8,128)(2,1)S(1)}, bf16[384,128]{1,0:T(8,128)(2,1)S(1)}, u32[]{:S(2)}, u32[]{:S(2)}) %collective-permute-start.24) | collective-permute-done | bytes 98336 | tf_op jit(solution)/shard_map/ppermute | solution.py:204
  121.0 5.9 %collective-permute-done.27 = bf16[2048,128]{1,0:T(8,128)(2,1)S(1)} collective-permute-done((bf16[2048,128]{1,0:T(8,128)(2,1)S(1)}, bf16[2048,128]{1,0:T(8,128)(2,1)S(1)}, u32[]{:S(2)}, u32[]{:S(2)}) %collective-permute-start.27) | collective-permute-done | bytes 524320 | tf_op jit(solution)/shard_map/ppermute | solution.py:306
  128.3 7.0 %collective-permute-start.28 = (bf16[2048,128]{1,0:T(8,128)(2,1)S(1)}, bf16[2048,128]{1,0:T(8,128)(2,1)S(1)}, u32[]{:S(2)}, u32[]{:S(2)}) collective-permute-start(bf16[2048,128]{1,0:T(8,128)(2,1)S(1)} %get-tuple-element.56), channel_id=1, source_target_pairs={{0,1},{1,2},{2,3},{4,5},{5,6},{6,7},{8,9},{9,10},{10,11},{12,13},{... | collective-permute-start | bytes 1572872 | tf_op jit(solution)/shard_map/ppermute | solution.py:306
  138.5 7.7 %collective-permute-start.37 = (bf16[2048,128]{1,0:T(8,128)(2,1)S(1)}, bf16[2048,128]{1,0:T(8,128)(2,1)}, u32[]{:S(2)}, u32[]{:S(2)}) collective-permute-start(bf16[2048,128]{1,0:T(8,128)(2,1)S(1)} %get-tuple-element.58), channel_id=1, source_target_pairs={{0,1},{1,2},{2,3},{4,5},{5,6},{6,7},{8,9},{9,10},{10,11},{12,13},{... | collective-permute-start | bytes 1572872 | tf_op jit(solution)/shard_map/ppermute | solution.py:306
  149.9 9.0 %collective-permute-done.37 = bf16[2048,128]{1,0:T(8,128)(2,1)} collective-permute-done((bf16[2048,128]{1,0:T(8,128)(2,1)S(1)}, bf16[2048,128]{1,0:T(8,128)(2,1)}, u32[]{:S(2)}, u32[]{:S(2)}) %collective-permute-start.37) | collective-permute-done | bytes 524320 | tf_op jit(solution)/shard_map/ppermute | solution.py:306
  161.0 2.0 %copy.21 = bf16[8,256,2,128]{3,2,1,0:T(2,128)(2,1)} copy(bf16[8,256,2,128]{1,3,2,0:T(8,128)(2,1)S(1)} %bitcast.117) | data formatting | bytes 2097152
  (138 shorter events, 50.8 us)
Async XLA Ops:
  10.1 11.4 %collective-permute-start.4 = (bf16[4,8,4096]{2,1,0:T(8,128)(2,1)}, bf16[4,8,4096]{2,1,0:T(8,128)(2,1)S(1)}, u32[]{:S(2)}, u32[]{:S(2)}) collective-permute-start(bf16[4,8,4096]{2,1,0:T(8,128)(2,1)} %get-tuple-element.30), channel_id=1, source_target_pairs={{0,4},{4,0},{8,12},{12,8},{16,20},{20,16},{24,28},{28,24},{1,5},{5... | collective-permute-start | bytes 786440 | tf_op jit(solution)/shard_map/ppermute | solution.py:204
  22.1 6.8 %collective-permute-start.6 = (bf16[8,5120]{1,0:T(8,128)(2,1)S(1)}, bf16[8,5120]{1,0:T(8,128)(2,1)S(1)}, u32[]{:S(2)}, u32[]{:S(2)}) collective-permute-start(bf16[8,5120]{1,0:T(8,128)(2,1)S(1)} %fusion.34), channel_id=1, source_target_pairs={{0,16},{4,20},{8,24},{12,28},{16,0},{20,4},{24,8},{28,12},{1,17},{... | collective-permute-start | bytes 245768 | tf_op jit(solution)/shard_map/ppermute | solution.py:204
  48.7 6.7 %collective-permute-start.12 = (bf16[256,128]{1,0:T(8,128)(2,1)S(1)}, bf16[256,128]{1,0:T(8,128)(2,1)S(1)}, u32[]{:S(2)}, u32[]{:S(2)}) collective-permute-start(bf16[256,128]{1,0:T(8,128)(2,1)S(1)} %get-tuple-element.75), channel_id=1, source_target_pairs={{0,1},{1,0},{2,3},{3,2},{4,5},{5,4},{6,7},{7,6},{8,9},{9,8},{10,11... | collective-permute-start | bytes 196616 | tf_op jit(solution)/shard_map/ppermute | solution.py:204
  50.4 6.6 %collective-permute-start.13 = (bf16[256,128]{1,0:T(8,128)(2,1)S(1)}, bf16[256,128]{1,0:T(8,128)(2,1)S(1)}, u32[]{:S(2)}, u32[]{:S(2)}) collective-permute-start(bf16[256,128]{1,0:T(8,128)(2,1)S(1)} %get-tuple-element.75), channel_id=1, source_target_pairs={{0,2},{1,3},{2,0},{3,1},{4,6},{5,7},{6,4},{7,5},{8,10},{9,11},{10,... | collective-permute-start | bytes 196616 | tf_op jit(solution)/shard_map/ppermute | solution.py:204
  53.0 6.1 %collective-permute-start.14 = (bf16[256,128]{1,0:T(8,128)(2,1)S(1)}, bf16[256,128]{1,0:T(8,128)(2,1)S(1)}, u32[]{:S(2)}, u32[]{:S(2)}) collective-permute-start(bf16[256,128]{1,0:T(8,128)(2,1)S(1)} %get-tuple-element.75), channel_id=1, source_target_pairs={{0,3},{1,2},{2,1},{3,0},{4,7},{5,6},{6,5},{7,4},{8,11},{9,10},{10,... | collective-permute-start | bytes 196616 | tf_op jit(solution)/shard_map/ppermute | solution.py:204
  53.2 7.2 %collective-permute-start.31 = (bf16[8,4096]{1,0:T(8,128)(2,1)S(1)}, bf16[8,4096]{1,0:T(8,128)(2,1)S(1)}, u32[]{:S(2)}, u32[]{:S(2)}) collective-permute-start(bf16[8,4096]{1,0:T(8,128)(2,1)S(1)} %fusion.41), channel_id=1, source_target_pairs={{0,8},{4,12},{8,0},{12,4},{16,24},{20,28},{24,16},{28,20},{1,9},{5... | collective-permute-start | bytes 196616 | tf_op jit(solution)/shard_map/ppermute | solution.py:204
  60.6 8.6 %collective-permute-start.34 = (bf16[4,8,4096]{2,1,0:T(8,128)(2,1)S(1)}, bf16[4,8,4096]{2,1,0:T(8,128)(2,1)S(1)}, u32[]{:S(2)}, u32[]{:S(2)}) collective-permute-start(bf16[4,8,4096]{2,1,0:T(8,128)(2,1)S(1)} %pad_maximum_fusion.4.refs_2_), channel_id=1, source_target_pairs={{0,4},{4,0},{8,12},{12,8},{16,20},{20,16},{24,28},{28,24},{1,5},{5... | collective-permute-start | bytes 786440 | tf_op jit(solution)/shard_map/ppermute | solution.py:204
  65.2 46.2 %collective-permute-start.26 = (bf16[2048,128]{1,0:T(8,128)(2,1)}, bf16[2048,128]{1,0:T(8,128)(2,1)}, u32[]{:S(2)}, u32[]{:S(2)}) collective-permute-start(bf16[2048,128]{1,0:T(8,128)(2,1)} %get-tuple-element.46), channel_id=1, source_target_pairs={{0,1},{3,2},{4,5},{7,6},{8,9},{11,10},{12,13},{15,14},{16,17},{19,... | collective-permute-start | bytes 1572872 | tf_op jit(solution)/shard_map/ppermute | solution.py:304
  69.1 16.6 %collective-permute-start.19 = (f32[256,128]{1,0:T(8,128)S(1)}, f32[256,128]{1,0:T(8,128)S(1)}, u32[]{:S(2)}, u32[]{:S(2)}) collective-permute-start(f32[256,128]{1,0:T(8,128)S(1)} %convert_add_fusion.3), channel_id=1, source_target_pairs={{0,4},{4,0},{8,12},{12,8},{16,20},{20,16},{24,28},{28,24},{1,5},{5... | collective-permute-start | bytes 393224 | tf_op jit(solution)/shard_map/ppermute | solution.py:204
  83.3 33.9 %collective-permute-start.35 = (bf16[2048,128]{1,0:T(8,128)(2,1)}, bf16[2048,128]{1,0:T(8,128)(2,1)}, u32[]{:S(2)}, u32[]{:S(2)}) collective-permute-start(bf16[2048,128]{1,0:T(8,128)(2,1)} %get-tuple-element.51), channel_id=1, source_target_pairs={{0,1},{3,2},{4,5},{7,6},{8,9},{11,10},{12,13},{15,14},{16,17},{19,... | collective-permute-start | bytes 1572872 | tf_op jit(solution)/shard_map/ppermute | solution.py:304
  90.1 9.3 %collective-permute-start.20 = (bf16[384,128]{1,0:T(8,128)(2,1)S(1)}, bf16[384,128]{1,0:T(8,128)(2,1)S(1)}, u32[]{:S(2)}, u32[]{:S(2)}) collective-permute-start(bf16[384,128]{1,0:T(8,128)(2,1)S(1)} %get-tuple-element.70), channel_id=1, source_target_pairs={{0,1},{1,0},{2,3},{3,2},{4,5},{5,4},{6,7},{7,6},{8,9},{9,8},{10,11... | collective-permute-start | bytes 294920 | tf_op jit(solution)/shard_map/ppermute | solution.py:204
  90.2 11.4 %collective-permute-start.21 = (bf16[384,128]{1,0:T(8,128)(2,1)S(1)}, bf16[384,128]{1,0:T(8,128)(2,1)S(1)}, u32[]{:S(2)}, u32[]{:S(2)}) collective-permute-start(bf16[384,128]{1,0:T(8,128)(2,1)S(1)} %get-tuple-element.72), channel_id=1, source_target_pairs={{0,2},{1,3},{2,0},{3,1},{4,6},{5,7},{6,4},{7,5},{8,10},{9,11},{10,... | collective-permute-start | bytes 294920 | tf_op jit(solution)/shard_map/ppermute | solution.py:204
  93.9 12.9 %collective-permute-start.22 = (bf16[384,128]{1,0:T(8,128)(2,1)S(1)}, bf16[384,128]{1,0:T(8,128)(2,1)S(1)}, u32[]{:S(2)}, u32[]{:S(2)}) collective-permute-start(bf16[384,128]{1,0:T(8,128)(2,1)S(1)} %get-tuple-element.71), channel_id=1, source_target_pairs={{0,3},{1,2},{2,1},{3,0},{4,7},{5,6},{6,5},{7,4},{8,11},{9,10},{10,... | collective-permute-start | bytes 294920 | tf_op jit(solution)/shard_map/ppermute | solution.py:204
  106.9 7.7 %collective-permute-start.23 = (bf16[384,128]{1,0:T(8,128)(2,1)S(1)}, bf16[384,128]{1,0:T(8,128)(2,1)S(1)}, u32[]{:S(2)}, u32[]{:S(2)}) collective-permute-start(bf16[384,128]{1,0:T(8,128)(2,1)S(1)} %fusion.30), channel_id=1, source_target_pairs={{0,3},{1,2},{2,1},{3,0},{4,7},{5,6},{6,5},{7,4},{8,11},{9,10},{10,... | collective-permute-start | bytes 294920 | tf_op jit(solution)/shard_map/ppermute | solution.py:204
  107.8 9.3 %collective-permute-start.24 = (bf16[384,128]{1,0:T(8,128)(2,1)S(1)}, bf16[384,128]{1,0:T(8,128)(2,1)S(1)}, u32[]{:S(2)}, u32[]{:S(2)}) collective-permute-start(bf16[384,128]{1,0:T(8,128)(2,1)S(1)} %fusion.30), channel_id=1, source_target_pairs={{0,2},{1,3},{2,0},{3,1},{4,6},{5,7},{6,4},{7,5},{8,10},{9,11},{10,... | collective-permute-start | bytes 294920 | tf_op jit(solution)/shard_map/ppermute | solution.py:204
  107.8 9.3 %collective-permute-start.25 = (bf16[384,128]{1,0:T(8,128)(2,1)S(1)}, bf16[384,128]{1,0:T(8,128)(2,1)S(1)}, u32[]{:S(2)}, u32[]{:S(2)}) collective-permute-start(bf16[384,128]{1,0:T(8,128)(2,1)S(1)} %fusion.30), channel_id=1, source_target_pairs={{0,1},{1,0},{2,3},{3,2},{4,5},{5,4},{6,7},{7,6},{8,9},{9,8},{10,11... | collective-permute-start | bytes 294920 | tf_op jit(solution)/shard_map/ppermute | solution.py:204
  112.6 14.3 %collective-permute-start.27 = (bf16[2048,128]{1,0:T(8,128)(2,1)S(1)}, bf16[2048,128]{1,0:T(8,128)(2,1)S(1)}, u32[]{:S(2)}, u32[]{:S(2)}) collective-permute-start(bf16[2048,128]{1,0:T(8,128)(2,1)S(1)} %add_convert_fusion.7), channel_id=1, source_target_pairs={{0,1},{1,2},{4,5},{5,6},{8,9},{9,10},{12,13},{13,14},{16,17},{17,1... | collective-permute-start | bytes 1572872 | tf_op jit(solution)/shard_map/ppermute | solution.py:306
  114.6 12.3 %collective-permute-start.29 = (bf16[2048,128]{1,0:T(8,128)(2,1)S(1)}, bf16[2048,128]{1,0:T(8,128)(2,1)S(1)}, u32[]{:S(2)}, u32[]{:S(2)}) collective-permute-start(bf16[2048,128]{1,0:T(8,128)(2,1)S(1)} %add_convert_fusion.7), channel_id=1, source_target_pairs={{2,1},{3,2},{6,5},{7,6},{10,9},{11,10},{14,13},{15,14},{18,17},{19... | collective-permute-start | bytes 1572872 | tf_op jit(solution)/shard_map/ppermute | solution.py:306
  118.6 19.6 %collective-permute-start.36 = (bf16[2048,128]{1,0:T(8,128)(2,1)S(1)}, bf16[2048,128]{1,0:T(8,128)(2,1)S(1)}, u32[]{:S(2)}, u32[]{:S(2)}) collective-permute-start(bf16[2048,128]{1,0:T(8,128)(2,1)S(1)} %add_convert_fusion.3), channel_id=1, source_target_pairs={{0,1},{1,2},{4,5},{5,6},{8,9},{9,10},{12,13},{13,14},{16,17},{17,1... | collective-permute-start | bytes 1572872 | tf_op jit(solution)/shard_map/ppermute | solution.py:306
  120.3 17.8 %collective-permute-start.38 = (bf16[2048,128]{1,0:T(8,128)(2,1)S(1)}, bf16[2048,128]{1,0:T(8,128)(2,1)S(1)}, u32[]{:S(2)}, u32[]{:S(2)}) collective-permute-start(bf16[2048,128]{1,0:T(8,128)(2,1)S(1)} %add_convert_fusion.3), channel_id=1, source_target_pairs={{2,1},{3,2},{6,5},{7,6},{10,9},{11,10},{14,13},{15,14},{18,17},{19... | collective-permute-start | bytes 1572872 | tf_op jit(solution)/shard_map/ppermute | solution.py:306
  128.3 21.1 %collective-permute-start.28 = (bf16[2048,128]{1,0:T(8,128)(2,1)S(1)}, bf16[2048,128]{1,0:T(8,128)(2,1)S(1)}, u32[]{:S(2)}, u32[]{:S(2)}) collective-permute-start(bf16[2048,128]{1,0:T(8,128)(2,1)S(1)} %get-tuple-element.56), channel_id=1, source_target_pairs={{0,1},{1,2},{2,3},{4,5},{5,6},{6,7},{8,9},{9,10},{10,11},{12,13},{... | collective-permute-start | bytes 1572872 | tf_op jit(solution)/shard_map/ppermute | solution.py:306
  135.3 14.0 %collective-permute-start.30 = (bf16[2048,128]{1,0:T(8,128)(2,1)S(1)}, bf16[2048,128]{1,0:T(8,128)(2,1)S(1)}, u32[]{:S(2)}, u32[]{:S(2)}) collective-permute-start(bf16[2048,128]{1,0:T(8,128)(2,1)S(1)} %get-tuple-element.57), channel_id=1, source_target_pairs={{1,0},{2,1},{3,2},{5,4},{6,5},{7,6},{9,8},{10,9},{11,10},{13,12},{... | collective-permute-start | bytes 1572872 | tf_op jit(solution)/shard_map/ppermute | solution.py:306
  138.5 20.4 %collective-permute-start.37 = (bf16[2048,128]{1,0:T(8,128)(2,1)S(1)}, bf16[2048,128]{1,0:T(8,128)(2,1)}, u32[]{:S(2)}, u32[]{:S(2)}) collective-permute-start(bf16[2048,128]{1,0:T(8,128)(2,1)S(1)} %get-tuple-element.58), channel_id=1, source_target_pairs={{0,1},{1,2},{2,3},{4,5},{5,6},{6,7},{8,9},{9,10},{10,11},{12,13},{... | collective-permute-start | bytes 1572872 | tf_op jit(solution)/shard_map/ppermute | solution.py:306
  146.2 12.8 %collective-permute-start.39 = (bf16[2048,128]{1,0:T(8,128)(2,1)S(1)}, bf16[2048,128]{1,0:T(8,128)(2,1)}, u32[]{:S(2)}, u32[]{:S(2)}) collective-permute-start(bf16[2048,128]{1,0:T(8,128)(2,1)S(1)} %get-tuple-element.59), channel_id=1, source_target_pairs={{1,0},{2,1},{3,2},{5,4},{6,5},{7,6},{9,8},{10,9},{11,10},{13,12},{... | collective-permute-start | bytes 1572872 | tf_op jit(solution)/shard_map/ppermute | solution.py:306
  (33 other events, 242.2 us)
